TPU v7x, 32 devices: a whole 2x2x4 slice. The times are simulated.
32 devices in a mesh: req: 16 (over z, y, x), blk: 2 (over core).
Axes of the slice: x: 2, y: 2, z: 4, core: 2. Of those that a mesh axis runs over, the one named last changes fastest.
Arguments:
- hidden: bfloat16 [16, 1600], P('req'), may hold values from -6 to 6
- slot_request: int32 [16], replicated, may hold values from 0 to 15, each once
- cache_length: int32 [16], P('req'), may hold values from 1 to 2048, 4096 in all
- block_keep: int32 [16, 16], P('req', 'blk'), may hold values 0 or 1
- stored_keys: bfloat16 [16, 2048, 320], P('req', 'blk'), may hold values from -540 to 540
- stored_values: bfloat16 [16, 2048, 320], P('req', 'blk'), may hold values from -6 to 6
- ssm_state: float32 [16, 16, 3200], P('req', None, 'blk'), may hold values from -6 to 6
- norm_gain: float32 [1600], replicated, may hold values from 0.5 to 1.5
- query_key_value_weight: bfloat16 [1600, 2240], P('blk'), may hold values from -0.15625 to 0.15625
- w_attn_out: bfloat16 [1600, 1600], P('blk'), may hold values from -0.15625 to 0.15625
- mamba_in: bfloat16 [2, 1600, 3200], P(None, None, 'blk'), may hold values from -0.15625 to 0.15625
- select_proj: bfloat16 [3200, 132], P('blk'), may hold values from -0.109375 to 0.109375
- step_proj: bfloat16 [100, 3200], P(None, 'blk'), may hold values from -0.625 to 0.625
- step_bias: float32 [3200], P('blk'), may hold values from -3 to 0.5
- decay_log: float32 [16, 3200], P(None, 'blk'), may hold values from 0 to 2.8
- skip_gain: float32 [3200], P('blk'), may hold values from 0.5 to 1.5
- w_mamba_out: bfloat16 [3200, 1600], P('blk'), may hold values from -0.109375 to 0.109375
- ffn_gain: float32 [1600], replicated, may hold values from 0.5 to 1.5
- w_gate_up: bfloat16 [2, 1600, 5504], P(None, None, 'blk'), may hold values from -0.15625 to 0.15625
- w_down: bfloat16 [5504, 1600], P('blk'), may hold values from -0.078125 to 0.078125
Outputs:
- hidden_out: bfloat16 [16, 1600], P('req', 'blk')
- fresh_entry: bfloat16 [16, 640], P('req')
- new_state: float32 [16, 16, 3200], P('req', None, 'blk')
Inputs may be any that keep to these rules, and one draw needn't show every extreme that they name: `slot_request`: each request stands in exactly one slot.
All inputs are finite; a program needn't handle non-finite values. No bound on the sum of `cache_length` or of `block_keep` on one device may be relied on, other than what follows from the above.
Results may differ from a plain program's by a relative error of at most 0.0085.
Values may be sent and summed in bfloat16 or wider, within the bound.
A program may use at most 128 MiB of HBM per device.

v0:
```python
import jax
import jax.numpy as jnp
from jax import lax
from jax.sharding import PartitionSpec as P

QUERY_HEADS = 25
HEAD_SIZE = 64
KEY_HEADS = 5
NS = 16
RANK = 100
BLOCK_POSITIONS = 128


epsilon = 1e-05
floor_score = -1e30


def merged(value, axis, join):
    pieces = jax.tree.map(lambda part: lax.all_gather(part, axis), value)
    head = jax.tree.map(lambda part: part[0], pieces)
    tail = jax.tree.map(lambda part: part[1:], pieces)
    running, _ = lax.scan(lambda running, share: (join(running, share), None), head, tail)
    return running


def rms_scale(block_values):
    return lax.rsqrt(jnp.mean(block_values * block_values, axis=-1, keepdims=True) + epsilon)


def merge_stats(first_block, second):
    max_first, sum_first, acc_first = first_block
    max_second, sum_second, acc_second = second
    top = jnp.maximum(max_first, max_second)
    scale_first = jnp.exp(max_first - top)
    scale_second = jnp.exp(max_second - top)
    total = sum_first * scale_first + sum_second * scale_second
    accum = acc_first * scale_first[..., None] + acc_second * scale_second[..., None]
    return (top, total, accum)


def per_device(
    hidden,
    slot_request,
    cache_length,
    block_keep,
    stored_keys,
    stored_values,
    ssm_state,
    norm_gain,
    query_key_value_weight,
    w_attn_out,
    mamba_in,
    select_proj,
    step_proj,
    step_bias,
    decay_log,
    skip_gain,
    w_mamba_out,
    ffn_gain,
    w_gate_up,
    w_down,
):
    request_shard = hidden.shape[0]
    blk_count = lax.axis_size("blk")
    blk_index = lax.axis_index("blk")
    grp_index = lax.axis_index("req")
    feat_dev = query_key_value_weight.shape[0]
    att_dev = w_attn_out.shape[0]
    att_width = att_dev * blk_count
    key_value_width = KEY_HEADS * HEAD_SIZE
    query_group = QUERY_HEADS // KEY_HEADS
    scale = HEAD_SIZE ** (-0.5)
    hidden_f = hidden.astype(jnp.float32)
    normed = (hidden_f * rms_scale(hidden_f) * norm_gain).astype(jnp.bfloat16)
    own_feat = lax.dynamic_slice_in_dim(normed, blk_index * feat_dev, feat_dev, 1)
    qkv_part = jnp.dot(own_feat, query_key_value_weight, preferred_element_type=jnp.float32)
    x_inner = jnp.dot(normed, mamba_in[0], preferred_element_type=jnp.float32)
    z_gate = jnp.dot(normed, mamba_in[1], preferred_element_type=jnp.float32)
    inner_act = jax.nn.silu(x_inner).astype(jnp.bfloat16)
    select_part = jnp.dot(inner_act, select_proj, preferred_element_type=jnp.float32)
    qkv_full, select_full = lax.psum((qkv_part, select_part), "blk")
    qkv_bf = qkv_full.astype(jnp.bfloat16)
    query_vector = qkv_bf[:, :att_width]
    fresh_entry = qkv_bf[:, att_width:]
    step_low = select_full[:, :RANK]
    in_gain = select_full[:, RANK : RANK + NS]
    out_gain = select_full[:, RANK + NS :]
    step_size = jax.nn.softplus(
        jnp.dot(step_low, step_proj.astype(jnp.float32), precision=lax.Precision.HIGHEST)
        + step_bias
    )
    rates = -jnp.exp(decay_log)
    decay = jnp.exp(step_size[:, None, :] * rates[None])
    inner_f = inner_act.astype(jnp.float32)
    new_state = decay * ssm_state + (step_size * inner_f)[:, None, :] * in_gain[:, :, None]
    ssm_out = jnp.sum(out_gain[:, :, None] * new_state, axis=1) + skip_gain * inner_f
    mamba_act = (ssm_out * jax.nn.silu(z_gate)).astype(jnp.bfloat16)
    blocks_shard = stored_keys.shape[1] // BLOCK_POSITIONS
    block_keys = stored_keys.reshape(
        request_shard, blocks_shard, BLOCK_POSITIONS, KEY_HEADS, HEAD_SIZE
    )
    block_values = stored_values.reshape(
        request_shard, blocks_shard, BLOCK_POSITIONS, KEY_HEADS, HEAD_SIZE
    )
    query_grouped4 = query_vector.reshape(request_shard, KEY_HEADS, query_group, HEAD_SIZE)
    scores = (
        jnp.einsum(
            "rkgd,rjpkd->rjkgp", query_grouped4, block_keys, preferred_element_type=jnp.float32
        )
        * scale
    )
    position = (
        blk_index * (blocks_shard * BLOCK_POSITIONS)
        + jnp.arange(blocks_shard, dtype=jnp.int32)[:, None] * BLOCK_POSITIONS
        + jnp.arange(BLOCK_POSITIONS, dtype=jnp.int32)[None, :]
    )
    valid = (position[None] < cache_length[:, None, None]) & (block_keep[:, :, None] == 1)
    valid5 = valid[:, :, None, None, :]
    masked = jnp.where(valid5, scores, floor_score)
    block_max = jnp.max(masked, axis=-1)
    weights = jnp.where(valid5, jnp.exp(masked - block_max[..., None]), 0.0)
    block_sum = jnp.sum(weights, axis=-1)
    block_acc = jnp.einsum(
        "rjkgp,rjpkd->rjkgd",
        weights.astype(jnp.bfloat16),
        block_values,
        preferred_element_type=jnp.float32,
    )
    local_max = jnp.max(block_max, axis=1)
    rescale = jnp.exp(block_max - local_max[:, None])
    local_sum = jnp.sum(block_sum * rescale, axis=1)
    local_acc = jnp.sum(block_acc * rescale[..., None], axis=1)
    top, total, accum = merged((local_max, local_sum, local_acc), "blk", merge_stats)
    fresh_key = fresh_entry[:, :key_value_width].reshape(request_shard, KEY_HEADS, HEAD_SIZE)
    fresh_value = (
        fresh_entry[:, key_value_width:]
        .astype(jnp.float32)
        .reshape(request_shard, KEY_HEADS, 1, HEAD_SIZE)
    )
    own_score = (
        jnp.einsum("rkgd,rkd->rkg", query_grouped4, fresh_key, preferred_element_type=jnp.float32)
        * scale
    )
    highest = jnp.maximum(top, own_score)
    old_scale = jnp.exp(top - highest)
    own_weight = jnp.exp(own_score - highest)
    total = total * old_scale + own_weight
    accum = accum * old_scale[..., None] + own_weight[..., None] * fresh_value
    attended = (accum / total[..., None]).reshape(request_shard, att_width).astype(jnp.bfloat16)
    own_att = lax.dynamic_slice_in_dim(attended, blk_index * att_dev, att_dev, 1)
    mix_term = 0.5 * (
        jnp.dot(own_att, w_attn_out, preferred_element_type=jnp.float32)
        + jnp.dot(mamba_act, w_mamba_out, preferred_element_type=jnp.float32)
    )
    mixed_rows = lax.psum(mix_term, "blk")
    resid = (hidden_f + mixed_rows).astype(jnp.bfloat16)
    resid_f = resid.astype(jnp.float32)
    ffn_in = (resid_f * rms_scale(resid_f) * ffn_gain).astype(jnp.bfloat16)
    gate = jnp.dot(ffn_in, w_gate_up[0], preferred_element_type=jnp.float32)
    upper = jnp.dot(ffn_in, w_gate_up[1], preferred_element_type=jnp.float32)
    ffn_hidden = (jax.nn.silu(gate) * upper).astype(jnp.bfloat16)
    down_part = jnp.dot(ffn_hidden, w_down, preferred_element_type=jnp.float32)
    targets = grp_index * request_shard + jnp.arange(request_shard, dtype=jnp.int32)
    picker = (slot_request[None, :] == targets[:, None]).astype(jnp.bfloat16)
    ffn_out = lax.psum(down_part, "blk")
    final_rows = (resid_f + ffn_out).astype(jnp.bfloat16)
    every_row = lax.all_gather(final_rows, "req", axis=0, tiled=True)
    columns = lax.dynamic_slice_in_dim(every_row, blk_index * feat_dev, feat_dev, 1)
    hidden_out = jnp.dot(picker, columns, preferred_element_type=jnp.float32).astype(jnp.bfloat16)
    return (hidden_out, fresh_entry, new_state)


def solution(mesh):
    return jax.shard_map(
        per_device,
        mesh=mesh,
        in_specs=(
            P("req", None),
            P(),
            P("req"),
            P("req", "blk"),
            P("req", "blk", None),
            P("req", "blk", None),
            P("req", None, "blk"),
            P(),
            P("blk", None),
            P("blk", None),
            P(None, None, "blk"),
            P("blk", None),
            P(None, "blk"),
            P("blk"),
            P(None, "blk"),
            P("blk"),
            P("blk", None),
            P(),
            P(None, None, "blk"),
            P("blk", None),
        ),
        out_specs=(P("req", "blk"), P("req", None), P("req", None, "blk")),
        check_vma=False,
    )
```

profile of v0, /device:TPU:0, one launch (start us, length us, event | category | flops | bytes accessed | tf_op | source)
XLA Modules:
  0.0 102.7 jit_solution(5238256751461600700)
XLA Ops:
  0.6 0.0 copy-start
  0.6 0.0 copy-start.1
  0.7 0.0 copy-start.3
  0.7 0.0 copy-start.4
  0.7 1.5 %multiply_reduce_fusion.3 = f32[]{:T(128)} fusion(bf16[1,1600]{1,0:T(2,128)(2,1)} %param.20), kind=kLoop, calls=%fused_computation.67 | loop fusion | flops 4799 | bytes 3204 | tf_op jit(solution)/shard_map/reduce_sum | solution.py:27
  2.9 0.0 copy-start.2
  2.9 0.8 multiply_convert_fusion.2
  3.7 3.3 %fusion.60 = f32[1,2240]{1,0:T(1,128)} fusion(bf16[800,2240]{1,0:T(8,128)(2,1)} %param.28, bf16[1,1600]{1,0:T(2,128)(2,1)S(1)} %multiply_convert_fusion.2, s32[]{:T(128)S(6)} %select_n.20), kind=kOutput, calls=%fused_computation.89 | convolution fusion | flops 3584000 | bytes 3596548 | tf_op jit(solution)/shard_map/dot_general | solution.py:76
  6.9 3.3 %fusion.16 = f32[1600]{0:T(1024)S(1)} fusion(bf16[2,1600,1600]{2,1,0:T(8,128)(2,1)} %param.30, bf16[1,1600]{1,0:T(2,128)(2,1)S(1)} %multiply_convert_fusion.2), kind=kOutput, calls=%fused_computation.22 | convolution fusion | flops 5120000 | bytes 5334400 | tf_op jit(solution)/shard_map/dot_general | solution.py:77
  10.3 0.0 copy-done.2
  10.3 0.2 fusion.75
  10.5 5.1 %all-reduce = (bf16[1,2240]{1,0:T(2,128)(2,1)}, f32[1,132]{1,0:T(1,128)S(1)}) all-reduce(f32[1,2240]{1,0:T(1,128)} %fusion.60, f32[1,132]{1,0:T(1,128)S(1)} %fusion.75), channel_id=1, replica_groups=mesh['req'=16,'blk'=2] {'blk'}, use_global_device_ids=true, to_apply=%region_1.2 | all-reduce | flops 2372 | bytes 14496 | tf_op jit(solution)/shard_map/psum | solution.py:81
  15.6 0.7 slice_reduce_fusion
  16.3 0.7 reshape.515
  17.7 0.7 compare_bitcast_fusion
  18.3 0.1 fusion.57
  18.4 0.0 copy-done.1
  18.4 0.1 copy.40
  18.5 0.0 copy-start.7
  18.6 0.0 copy-start.5
  18.6 0.0 copy-start.6
  18.6 1.0 fusion.73
  19.6 0.2 fusion.30
  19.8 1.8 %all-gather.4 = f32[2,5,5]{2,1,0:T(8,128)S(1)} all-gather(f32[1,5,5]{2,1,0:T(8,128)S(1)} %bitcast.149), channel_id=4, replica_groups=mesh['req'=16,'blk'=2] {'blk'}, dimensions={0}, use_global_device_ids=true | all-gather | bytes 300 | tf_op jit(solution)/shard_map/all_gather | solution.py:19
  21.6 1.8 %all-gather.3 = f32[2,5,5]{2,1,0:T(8,128)S(1)} all-gather(f32[1,5,5]{2,1,0:T(8,128)S(1)} %bitcast.148), channel_id=3, replica_groups=mesh['req'=16,'blk'=2] {'blk'}, dimensions={0}, use_global_device_ids=true | all-gather | bytes 300 | tf_op jit(solution)/shard_map/all_gather | solution.py:19
  23.4 0.1 reshape.470
  23.5 0.8 slice_reduce_fusion.1
  24.3 0.1 reshape.542
  24.3 0.1 fusion.74
  24.5 1.2 %copy.41 = bf16[40,8,8,128]{3,2,1,0:T(8,128)(2,1)S(1)} copy(bf16[40,8,8,128]{3,1,2,0:T(8,128)(2,1)} %bitcast.146) | data formatting | bytes 1310720
  25.7 0.4 fusion.15
  26.2 1.8 %all-gather = f32[10,5,64]{2,1,0:T(8,128)S(1)} all-gather(f32[5,5,64]{2,1,0:T(8,128)S(1)} %fusion.15), channel_id=2, replica_groups=mesh['req'=16,'blk'=2] {'blk'}, dimensions={0}, use_global_device_ids=true | all-gather | bytes 19200 | tf_op jit(solution)/shard_map/all_gather | solution.py:19
  28.0 0.7 fusion.66
  28.7 0.1 reshape.479
  28.8 0.1 fusion.39
  28.9 0.1 reshape.512
  29.0 0.0 copy-done
  29.0 0.5 convolution_reduce_fusion.2
  29.5 1.3 %convolution_reduce_fusion.1 = f32[1600]{0:T(1024)S(1)} fusion(bf16[100,1600]{1,0:T(8,128)(2,1)} %param.32, f32[1,132]{1,0:T(1,128)S(1)} %get-tuple-element.20), kind=kOutput, calls=%fused_computation.19 | convolution fusion | flops 1920000 | bytes 326912 | tf_op jit(solution)/shard_map/dot_general | solution.py:89
  30.8 0.7 convert_multiply_fusion.1
  31.5 0.1 slice_bitcast_fusion.4
  31.6 0.0 copy-done.3
  31.6 0.0 copy-done.4
  31.6 0.7 multiply_reduce_fusion
  32.3 3.3 %fusion.19 = f32[1600]{0:T(1024)S(1)} fusion(bf16[2,1600,1600]{2,1,0:T(8,128)(2,1)} %param.30, bf16[1,1600]{1,0:T(2,128)(2,1)S(1)} %multiply_convert_fusion.2), kind=kOutput, calls=%fused_computation.23 | convolution fusion | flops 5120000 | bytes 5334400 | tf_op jit(solution)/shard_map/dot_general | solution.py:78
  35.6 0.0 copy-done.7
  35.7 3.3 %convolution_reduce_fusion = f32[1600]{0:T(1024)S(1)} fusion(bf16[1600,1]{0,1:T(2,128)(2,1)S(1)} %reshape.528, bf16[1600,1600]{1,0:T(8,128)(2,1)} %param.36), kind=kOutput, calls=%fused_computation.18 | convolution fusion | flops 5120000 | bytes 5129600 | tf_op jit(solution)/shard_map/dot_general | solution.py:153
  39.0 2.5 %psum.30 = f32[1,1600]{1,0:T(1,128)S(1)} all-reduce(f32[1,1600]{1,0:T(1,128)S(1)} %mul.321), channel_id=1, replica_groups=mesh['req'=16,'blk'=2] {'blk'}, use_global_device_ids=true, to_apply=%region_9.10 | all-reduce | flops 1600 | bytes 12800 | tf_op jit(solution)/shard_map/psum | solution.py:155
  41.5 0.6 multiply_reduce_fusion.2
  42.8 0.0 copy-done.6
  42.8 0.0 slice-start
  42.8 0.0 slice-start.1
  42.8 5.0 %fusion.22 = f32[2752]{0:T(1024)S(1)} fusion(bf16[2,1600,2752]{2,1,0:T(8,128)(2,1)} %param.38, f32[1600]{0:T(1024)S(1)} %copy-done.6, bf16[1,1600]{1,0:T(2,128)(2,1)S(1)} %get-tuple-element.29, f32[]{:T(128)S(6)} %rsqrt.9), kind=kOutput, calls=%fused_computation.24 | convolution fusion | flops 8812800 | bytes 9031812 | tf_op jit(solution)/shard_map/dot_general | solution.py:159
  47.9 0.0 slice-start.2
  47.9 0.0 copy-start.8
  47.9 4.9 %fusion.25 = f32[2752]{0:T(1024)S(1)} fusion(bf16[2,1600,2752]{2,1,0:T(8,128)(2,1)} %param.38, f32[1600]{0:T(1024)S(1)} %copy-done.6, bf16[1,1600]{1,0:T(2,128)(2,1)S(1)} %get-tuple-element.29, f32[]{:T(128)S(6)} %rsqrt.9), kind=kOutput, calls=%fused_computation.25 | convolution fusion | flops 8812800 | bytes 9031812 | tf_op jit(solution)/shard_map/dot_general | solution.py:160
  52.9 2.4 %fusion.76 = f32[1,1600]{1,0:T(1,128)S(1)} fusion(bf16[2752,1]{0,1:T(2,128)(2,1)S(1)} %reshape.534, bf16[2752,1600]{0,1:T(8,128)(2,1)S(1)} %bitcast.143), kind=kOutput, calls=%fused_computation.110 | convolution fusion | flops 8806400 | bytes 8818304 | tf_op jit(solution)/shard_map/dot_general | solution.py:162
  55.3 2.5 %psum.31 = f32[1,1600]{1,0:T(1,128)S(1)} all-reduce(f32[1,1600]{1,0:T(1,128)S(1)} %fusion.76), channel_id=1, replica_groups=mesh['req'=16,'blk'=2] {'blk'}, use_global_device_ids=true, to_apply=%region_11.12 | all-reduce | flops 1600 | bytes 12800 | tf_op jit(solution)/shard_map/psum | solution.py:165
  57.8 42.7 %all-gather.5 = bf16[16,1,1600]{2,1,0:T(2,128)(2,1)S(1)} all-gather(bf16[1,1,1600]{2,1,0:T(2,128)(2,1)S(1)} %convert_bitcast_fusion), channel_id=1, replica_groups=mesh['req'=16,'blk'=2] {'req'}, dimensions={0}, use_global_device_ids=true | all-gather | bytes 54400 | tf_op jit(solution)/shard_map/all_gather | solution.py:167
  100.5 0.1 constant_dynamic-slice_fusion
  100.6 0.0 copy-done.8
  100.6 0.1 convolution_reduce_fusion.3
  100.8 0.6 convert_element_type.74
  101.4 1.3 %slice.95 = bf16[1,640]{1,0:T(2,128)(2,1)} slice(bf16[1,2240]{1,0:T(2,128)(2,1)} %get-tuple-element.19), slice={[0:1], [1600:2240]} | slice | bytes 2560 | tf_op jit(solution)/shard_map/slice | solution.py:84
  (18 shorter events, 0.1 us)
Async XLA Ops:
  0.6 28.3 %copy-start = (bf16[800,1600]{1,0:T(8,128)(2,1)S(1)}, bf16[800,1600]{1,0:T(8,128)(2,1)}, u32[]{:S(2)}) copy-start(bf16[800,1600]{1,0:T(8,128)(2,1)} %param.29) | copy-start | bytes 7680004
  0.6 17.8 %copy-start.1 = (bf16[1,1024,320]{1,2,0:T(8,128)(2,1)S(1)}, bf16[1,1024,320]{1,2,0:T(8,128)(2,1)}, u32[]{:S(2)}) copy-start(bf16[1,1024,320]{1,2,0:T(8,128)(2,1)} %param.24) | copy-start | bytes 1966084
  0.7 30.9 %copy-start.3 = (f32[1,16,1600]{2,1,0:T(8,128)S(1)}, f32[1,16,1600]{2,1,0:T(8,128)}, u32[]{:S(2)}) copy-start(f32[1,16,1600]{2,1,0:T(8,128)} %param.26) | copy-start | bytes 307204
  0.7 30.9 %copy-start.4 = (f32[16,1600]{1,0:T(8,128)S(1)}, f32[16,1600]{1,0:T(8,128)}, u32[]{:S(2)}) copy-start(f32[16,1600]{1,0:T(8,128)} %param.34) | copy-start | bytes 307204
  2.9 7.4 %copy-start.2 = (bf16[1600,132]{0,1:T(8,128)(2,1)S(1)}, bf16[1600,132]{0,1:T(8,128)(2,1)}, u32[]{:S(2)}) copy-start(bf16[1600,132]{0,1:T(8,128)(2,1)} %param.31) | copy-start | bytes 1267204
  18.5 17.1 %copy-start.7 = (f32[1600]{0:T(1024)S(1)}, f32[1600]{0:T(1024)}, u32[]{:S(2)}) copy-start(f32[1600]{0:T(1024)} %param.35) | copy-start | bytes 19204
  18.6 23.0 %copy-start.5 = (bf16[1,1600]{1,0:T(2,128)(2,1)S(1)}, bf16[1,1600]{1,0:T(2,128)(2,1)}, u32[]{:S(2)}) copy-start(bf16[1,1600]{1,0:T(2,128)(2,1)} %param.20) | copy-start | bytes 9604
  18.6 24.2 %copy-start.6 = (f32[1600]{0:T(1024)S(1)}, f32[1600]{0:T(1024)}, u32[]{:S(2)}) copy-start(f32[1600]{0:T(1024)} %param.37) | copy-start | bytes 19204
  42.8 10.0 %slice-start = ((s8[9011200]{0:T(1024)(128)(4,1)}), s8[4194304]{0:T(1024)(128)(4,1)S(1)}, s32[]{:S(2)}) async-start(s8[9011200]{0:T(1024)(128)(4,1)} %bitcast.142), calls=%async_computation | async-start | bytes 8388608
  42.8 10.0 %slice-start.1 = ((s8[9011200]{0:T(1024)(128)(4,1)}), s8[4194304]{0:T(1024)(128)(4,1)S(1)}, s32[]{:S(2)}) async-start(s8[9011200]{0:T(1024)(128)(4,1)} %bitcast.142), calls=%async_computation.1 | async-start | bytes 8388608
  47.9 5.0 %slice-start.2 = ((s8[9011200]{0:T(1024)(128)(4,1)}), s8[622592]{0:T(1024)(128)(4,1)S(1)}, s32[]{:S(2)}) async-start(s8[9011200]{0:T(1024)(128)(4,1)} %bitcast.142), calls=%async_computation.2 | async-start | bytes 1245184
  47.9 52.8 %copy-start.8 = (s32[16]{0:T(128)S(1)}, s32[16]{0:T(128)}, u32[]{:S(2)}) copy-start(s32[16]{0:T(128)} %param.21) | copy-start | bytes 196
where the time goes:
time: 103 us
  blocking collectives  58.2 us (57%)
  matrix products  29.2 us (28%)
  other arithmetic  6.16 us (6%)
  local copies, waits for them, and re-layouts  6.05 us (6%)
  between operations  3.02 us (3%)
    all_gather x1, blocking collectives, per_device(): every_row = lax.all_gather(final_rows, 'req', axis=0, tiled=True)  42.7 us
    all_gather x3, blocking collectives, merged(): pieces = jax.tree.map(lambda part: lax.all_gather(part, axis), value)  5.41 us
    psum x1, blocking collectives, per_device(): qkv_full, select_full = lax.psum((qkv_part, select_part), 'blk')  5.11 us
    dot_general x1, matrix products, per_device(): gate = jnp.dot(ffn_in, w_gate_up[0], preferred_element_type=jnp.float32)  5 us
    dot_general x1, matrix products, per_device(): upper = jnp.dot(ffn_in, w_gate_up[1], preferred_element_type=jnp.float32)  4.91 us
    dot_general x1, matrix products, per_device(): jnp.dot(mamba_act, w_mamba_out, preferred_element_type=jnp.float32)  3.31 us
    dot_general x1, matrix products, per_device(): x_inner = jnp.dot(normed, mamba_in[0], preferred_element_type=jnp.float32)  3.31 us
    dot_general x1, matrix products, per_device(): z_gate = jnp.dot(normed, mamba_in[1], preferred_element_type=jnp.float32)  3.31 us

commit v1 on v0

v1 whole, which is shorter than its diff:
```python
from functools import partial

import jax
import jax.numpy as jnp
from jax import lax
from jax.experimental import pallas as pl
from jax.experimental.pallas import tpu as pltpu
from jax.sharding import PartitionSpec as P

QUERY_HEADS = 25
HEAD_SIZE = 64
KEY_HEADS = 5
NS = 16
RANK = 100
BLOCK_POSITIONS = 128


epsilon = 1e-05
floor_score = -1e30

MESH = pl.DeviceIdType.MESH
VMEM_BYTES = 60 * 1024 * 1024
ROWS = 16
HEAD_ROWS = 32
STAT_LANES = 512


def rms_scale(block_values):
    return lax.rsqrt(jnp.mean(block_values * block_values, axis=-1, keepdims=True) + epsilon)


def silu(value):
    return value * jax.nn.sigmoid(value)


def bdot(left, right):
    return jnp.dot(left, right, preferred_element_type=jnp.float32)


def row_dot(row, weight):
    tall = jnp.broadcast_to(row, (ROWS, row.shape[1]))
    return bdot(tall, weight)[0:1]


def cuts_of(total, step):
    edges = list(range(0, total, step)) + [total]
    if len(edges) > 2 and edges[-1] - edges[-2] < step // 2:
        edges.pop(-2)
    return list(zip(edges[:-1], edges[1:]))


def own_part(value, index, count):
    width = value.shape[1] // count
    part = value[:, :width]
    for other in range(1, count):
        part = jnp.where(index == other, value[:, other * width : (other + 1) * width], part)
    return part


def send_all(buf, send_sem, recv_sem, stage, count):
    me = lax.axis_index("blk")
    copies = []
    for k in range(1, count):
        target = lax.rem(me + k, count)
        copy = pltpu.make_async_remote_copy(
            src_ref=buf.at[me],
            dst_ref=buf.at[me],
            send_sem=send_sem.at[stage, k],
            recv_sem=recv_sem.at[stage, me],
            device_id={"blk": target},
            device_id_type=MESH,
        )
        copy.start()
        copies.append(copy)
    return copies


def wait_all(copies, buf, send_sem, recv_sem, stage, count):
    me = lax.axis_index("blk")
    for k in range(1, count):
        source = lax.rem(me + k, count)
        pltpu.make_async_remote_copy(
            src_ref=buf.at[source],
            dst_ref=buf.at[source],
            send_sem=send_sem.at[stage, k],
            recv_sem=recv_sem.at[stage, source],
            device_id={"blk": source},
            device_id_type=MESH,
        ).wait_recv()
    for copy in copies:
        copy.wait_send()


def total_of(buf, count):
    result = buf[0]
    for k in range(1, count):
        result = result + buf[k]
    return result


def branch_kernel(
    count,
    hidden_ref,
    length_ref,
    keep_ref,
    state_ref,
    norm_ref,
    bias_ref,
    decay_ref,
    skip_ref,
    keys_hbm,
    values_hbm,
    qkv_hbm,
    attn_hbm,
    mamba_hbm,
    select_hbm,
    step_hbm,
    out_hbm,
    resid_ref,
    fresh_ref,
    new_state_ref,
    keys_ref,
    values_ref,
    qkv_w,
    attn_w,
    mamba_w,
    select_w,
    step_w,
    out_w,
    qkv_buf,
    sel_buf,
    stat_buf,
    mix_buf,
    load_sem,
    send_sem,
    recv_sem,
):
    me = lax.axis_index("blk")
    width = hidden_ref.shape[1]
    channels = state_ref.shape[2]
    positions = keys_ref.shape[0]
    key_width = KEY_HEADS * HEAD_SIZE
    group = QUERY_HEADS // KEY_HEADS
    att_width = QUERY_HEADS * HEAD_SIZE
    loads = []

    def load(source, target):
        copy = pltpu.make_async_copy(source, target, load_sem.at[len(loads)])
        copy.start()
        loads.append(copy)
        return copy

    feat_cuts = cuts_of(width, 512)
    load_qkv = load(qkv_hbm, qkv_w)
    load_x = [load(mamba_hbm.at[0, a:b], mamba_w.at[0, a:b]) for a, b in feat_cuts]
    load_select = load(select_hbm, select_w)
    load_keys = load(keys_hbm.at[0], keys_ref)
    load_values = load(values_hbm.at[0], values_ref)
    load_z = [load(mamba_hbm.at[1, a:b], mamba_w.at[1, a:b]) for a, b in feat_cuts]
    load_step = load(step_hbm, step_w)
    chan_cuts = cuts_of(channels, 512)
    load_out = [load(out_hbm.at[a:b], out_w.at[a:b]) for a, b in chan_cuts]
    load_attn = load(attn_hbm, attn_w)

    barrier = pltpu.get_barrier_semaphore()
    for k in range(1, count):
        pl.semaphore_signal(
            barrier, inc=1, device_id={"blk": lax.rem(me + k, count)}, device_id_type=MESH
        )
    pl.semaphore_wait(barrier, count - 1)

    hidden_f = hidden_ref[...].astype(jnp.float32)
    normed_f = hidden_f * rms_scale(hidden_f) * norm_ref[...].reshape(1, width)
    own_feat = own_part(normed_f, me, count).astype(jnp.bfloat16)
    normed = normed_f.astype(jnp.bfloat16)

    load_qkv.wait()
    qkv_buf[me] = row_dot(own_feat, qkv_w[...])
    sent_qkv = send_all(qkv_buf, send_sem, recv_sem, 0, count)

    def feature_dot(which, waits):
        result = jnp.zeros((1, channels), jnp.float32)
        for (a, b), wait in zip(feat_cuts, waits):
            wait.wait()
            result = result + row_dot(normed[:, a:b], mamba_w[which, a:b])
        return result

    inner_act = silu(feature_dot(0, load_x)).astype(jnp.bfloat16)
    inner_f = inner_act.astype(jnp.float32)
    load_select.wait()
    sel_buf[me] = row_dot(inner_act, select_w[...])
    sent_sel = send_all(sel_buf, send_sem, recv_sem, 1, count)

    wait_all(sent_qkv, qkv_buf, send_sem, recv_sem, 0, count)
    qkv_f = total_of(qkv_buf, count).astype(jnp.bfloat16).astype(jnp.float32)
    fresh_ref[...] = qkv_f[:, att_width:].astype(jnp.bfloat16)
    query = qkv_f[:, :att_width]
    new_key = qkv_f[:, att_width : att_width + key_width]
    new_value = qkv_f[:, att_width + key_width :]

    def owner_column(flat):
        head_group = jnp.zeros_like(flat)
        for g in range(1, KEY_HEADS):
            head_group = head_group + (flat >= g * group * HEAD_SIZE).astype(jnp.int32)
        return head_group * HEAD_SIZE + (flat & (HEAD_SIZE - 1))

    flat_rows = lax.broadcasted_iota(jnp.int32, (att_width, key_width), 0)
    flat_cols = lax.broadcasted_iota(jnp.int32, (att_width, key_width), 1)
    spread = (owner_column(flat_rows) == flat_cols).astype(jnp.float32).astype(jnp.bfloat16)
    head_of = lax.broadcasted_iota(jnp.int32, (HEAD_ROWS, att_width), 0)
    head_lane = lax.broadcasted_iota(jnp.int32, (HEAD_ROWS, att_width), 1)
    query_rows = jnp.where(head_of == (head_lane >> 6), jnp.broadcast_to(query, head_of.shape), 0.0)
    query_f = bdot(query_rows.astype(jnp.bfloat16), spread)
    query_bf = query_f.astype(jnp.bfloat16)

    scale = HEAD_SIZE ** (-0.5)
    load_keys.wait()
    scores = (
        lax.dot_general(
            query_bf, keys_ref[...], (((1,), (1,)), ((), ())), preferred_element_type=jnp.float32
        )
        * scale
    )
    lane = lax.broadcasted_iota(jnp.int32, (1, positions), 1)
    kept = jnp.zeros((1, positions), jnp.int32)
    for j in range(positions // BLOCK_POSITIONS):
        kept = jnp.where((lane >> 7) == j, keep_ref[0, j], kept)
    limit = length_ref[0] - me * positions
    live = jnp.where(lane < limit, kept, 0) == 1
    live = jnp.broadcast_to(live, scores.shape)
    masked = jnp.where(live, scores, floor_score)
    local_max = jnp.max(masked, axis=-1, keepdims=True)
    weights = jnp.where(live, jnp.exp(masked - local_max), 0.0)
    local_sum = jnp.sum(weights, axis=-1, keepdims=True)
    load_values.wait()
    stat_buf[me, :, :key_width] = bdot(weights.astype(jnp.bfloat16), values_ref[...])
    stat_lane = lax.broadcasted_iota(jnp.int32, (HEAD_ROWS, 128), 1)
    stat_buf[me, :, STAT_LANES - 128 :] = jnp.where(stat_lane < 64, local_max, local_sum)
    sent_stat = send_all(stat_buf, send_sem, recv_sem, 2, count)

    z_act = silu(feature_dot(1, load_z))

    wait_all(sent_sel, sel_buf, send_sem, recv_sem, 1, count)
    select_full = total_of(sel_buf, count)
    low = select_full[:, :RANK]
    low_a = low.astype(jnp.bfloat16).astype(jnp.float32)
    low_b = (low - low_a).astype(jnp.bfloat16).astype(jnp.float32)
    low_c = low - low_a - low_b
    term = lax.broadcasted_iota(jnp.int32, (ROWS, RANK), 0)
    terms = jnp.where(term == 0, low_a, jnp.where(term == 1, low_b, jnp.where(term == 2, low_c, 0.0)))
    load_step.wait()
    step_rows = bdot(terms.astype(jnp.bfloat16), step_w[...])
    raw = step_rows[0:1] + step_rows[1:2] + step_rows[2:3] + bias_ref[...].reshape(1, channels)
    step_size = jnp.maximum(raw, 0.0) + jnp.log1p(jnp.exp(-jnp.abs(raw)))

    gain_rows = lax.broadcasted_iota(jnp.int32, (NS, RANK + 2 * NS), 0)
    gain_lane = lax.broadcasted_iota(jnp.int32, (NS, RANK + 2 * NS), 1)
    select_rows = jnp.broadcast_to(select_full, gain_rows.shape)
    in_gain = jnp.sum(
        jnp.where(gain_lane == gain_rows + RANK, select_rows, 0.0), axis=1, keepdims=True
    )
    out_gain = jnp.sum(
        jnp.where(gain_lane == gain_rows + (RANK + NS), select_rows, 0.0), axis=1, keepdims=True
    )
    decay = jnp.exp(-step_size * jnp.exp(decay_ref[...]))
    new_state = decay * state_ref[0] + (step_size * inner_f) * in_gain
    new_state_ref[0] = new_state
    ssm_out = jnp.sum(out_gain * new_state, axis=0, keepdims=True)
    ssm_out = ssm_out + skip_ref[...].reshape(1, channels) * inner_f
    mamba_act = (ssm_out * z_act).astype(jnp.bfloat16)
    mix = jnp.zeros((1, width), jnp.float32)
    for (a, b), wait in zip(chan_cuts, load_out):
        wait.wait()
        mix = mix + row_dot(mamba_act[:, a:b], out_w[a:b])

    wait_all(sent_stat, stat_buf, send_sem, recv_sem, 2, count)
    own_score = jnp.sum(query_f * new_key, axis=-1, keepdims=True) * scale
    highest = own_score
    for k in range(count):
        highest = jnp.maximum(highest, stat_buf[k, :, STAT_LANES - 128 : STAT_LANES - 127])
    total = jnp.zeros_like(own_score)
    accum = jnp.zeros((HEAD_ROWS, key_width), jnp.float32)
    for k in range(count):
        factor = jnp.exp(stat_buf[k, :, STAT_LANES - 128 : STAT_LANES - 127] - highest)
        total = total + stat_buf[k, :, STAT_LANES - 64 : STAT_LANES - 63] * factor
        accum = accum + stat_buf[k, :, :key_width] * factor
    own_weight = jnp.exp(own_score - highest)
    total = total + own_weight
    accum = accum + own_weight * new_value
    attended = accum / total
    att_rows = lax.broadcasted_iota(jnp.int32, attended.shape, 0)
    att_cols = lax.broadcasted_iota(jnp.int32, attended.shape, 1) >> 6
    att_group = jnp.zeros_like(att_rows)
    for g in range(1, KEY_HEADS):
        att_group = att_group + (att_rows >= g * group).astype(jnp.int32)
    attended = jnp.where(att_group == att_cols, attended, 0.0).astype(jnp.bfloat16)
    part = att_width // count
    gather_rows = lax.broadcasted_iota(jnp.int32, (key_width, part), 0)
    gather_cols = lax.broadcasted_iota(jnp.int32, (key_width, part), 1) + me * part
    gather = (owner_column(gather_cols) == gather_rows).astype(jnp.float32).astype(jnp.bfloat16)
    att_flat = bdot(attended, gather)
    flat_head = lax.broadcasted_iota(jnp.int32, (HEAD_ROWS, part), 0)
    flat_lane = (lax.broadcasted_iota(jnp.int32, (HEAD_ROWS, part), 1) + me * part) >> 6
    own_att = jnp.sum(jnp.where(flat_head == flat_lane, att_flat, 0.0), axis=0, keepdims=True)
    load_attn.wait()
    mix = mix + row_dot(own_att.astype(jnp.bfloat16), attn_w[...])
    mix_buf[me] = 0.5 * mix
    sent_mix = send_all(mix_buf, send_sem, recv_sem, 3, count)
    wait_all(sent_mix, mix_buf, send_sem, recv_sem, 3, count)
    resid_ref[...] = (hidden_f + total_of(mix_buf, count)).astype(jnp.bfloat16)


def mix_branches(
    hidden, cache_length, block_keep, stored_keys, stored_values, ssm_state, norm_gain,
    query_key_value_weight, w_attn_out, mamba_in, select_proj, step_proj, step_bias, decay_log,
    skip_gain, w_mamba_out,
):
    count = lax.axis_size("blk")
    width = hidden.shape[1]
    channels = ssm_state.shape[2]
    qkv_width = query_key_value_weight.shape[1]
    vmem = pl.BlockSpec(memory_space=pltpu.VMEM)
    smem = pl.BlockSpec(memory_space=pltpu.SMEM)
    hbm = pl.BlockSpec(memory_space=pl.ANY)
    big = (query_key_value_weight, w_attn_out, mamba_in, select_proj, step_proj, w_mamba_out)
    return pl.pallas_call(
        partial(branch_kernel, count),
        out_shape=(
            jax.ShapeDtypeStruct(hidden.shape, jnp.bfloat16),
            jax.ShapeDtypeStruct((1, 2 * KEY_HEADS * HEAD_SIZE), jnp.bfloat16),
            jax.ShapeDtypeStruct(ssm_state.shape, jnp.float32),
        ),
        in_specs=[vmem, smem, smem, vmem, vmem, vmem, vmem, vmem] + [hbm] * 8,
        out_specs=(vmem, vmem, vmem),
        scratch_shapes=[
            pltpu.VMEM(stored_keys.shape[1:], jnp.bfloat16),
            pltpu.VMEM(stored_values.shape[1:], jnp.bfloat16),
        ]
        + [pltpu.VMEM(w.shape, w.dtype) for w in big]
        + [
            pltpu.VMEM((count, 1, qkv_width), jnp.float32),
            pltpu.VMEM((count, 1, select_proj.shape[1]), jnp.float32),
            pltpu.VMEM((count, HEAD_ROWS, STAT_LANES), jnp.float32),
            pltpu.VMEM((count, 1, width), jnp.float32),
            pltpu.SemaphoreType.DMA((32,)),
            pltpu.SemaphoreType.DMA((4, count)),
            pltpu.SemaphoreType.DMA((4, count)),
        ],
        compiler_params=pltpu.CompilerParams(
            collective_id=0, has_side_effects=True, vmem_limit_bytes=VMEM_BYTES
        ),
    )(
        hidden, cache_length, block_keep, ssm_state, norm_gain, step_bias, decay_log, skip_gain,
        stored_keys, stored_values, *big,
    )


def ffn_kernel(
    groups, count, tile, hidden_units,
    resid_ref, gain_ref, slot_ref, gate_up_ref, down_ref,
    out_ref,
    row_buf, rows_ref, part_buf, take_buf, row_send, row_recv, part_send, part_recv,
):
    devices = groups * count
    grp = lax.axis_index("req")
    blk = lax.axis_index("blk")
    me = grp * count + blk
    width = resid_ref.shape[1]
    half = width // count

    barrier = pltpu.get_barrier_semaphore()

    @pl.loop(1, devices)
    def _(k):
        target = lax.rem(me + k, devices)
        pl.semaphore_signal(
            barrier,
            inc=1,
            device_id=(target // count, lax.rem(target, count)),
            device_id_type=MESH,
        )

    row_buf[grp] = resid_ref[...].astype(jnp.float32)
    pl.semaphore_wait(barrier, devices - 1)

    def row_copy(k, slot, peer):
        return pltpu.make_async_remote_copy(
            src_ref=row_buf.at[slot],
            dst_ref=row_buf.at[slot],
            send_sem=row_send.at[k],
            recv_sem=row_recv.at[slot],
            device_id=(peer, blk),
            device_id_type=MESH,
        )

    @pl.loop(1, groups)
    def _(k):
        row_copy(k, grp, lax.rem(grp + k, groups)).start()

    @pl.loop(1, groups)
    def _(k):
        peer = lax.rem(grp + k, groups)
        row_copy(k, peer, peer).wait_recv()

    for r in range(groups):
        rows_ref[r : r + 1, :] = row_buf[r]
    resid_f = rows_ref[...]
    ffn_in = (resid_f * rms_scale(resid_f) * gain_ref[...].reshape(1, width)).astype(jnp.bfloat16)
    gate = bdot(ffn_in, gate_up_ref[0])
    upper = bdot(ffn_in, gate_up_ref[1])
    unit = grp * tile + lax.broadcasted_iota(jnp.int32, (groups, tile), 1)
    ffn_hidden = jnp.where(unit < hidden_units, silu(gate) * upper, 0.0).astype(jnp.bfloat16)
    lane = lax.broadcasted_iota(jnp.int32, (groups, groups), 1)
    slots = jnp.zeros((groups, groups), jnp.int32)
    for s in range(groups):
        slots = jnp.where(lane == s, slot_ref[s], slots)
    request = lax.broadcasted_iota(jnp.int32, (groups, groups), 0)
    picker = (slots == request).astype(jnp.float32).astype(jnp.bfloat16)
    placed = bdot(picker, ffn_hidden).astype(jnp.bfloat16)
    weight_unit = grp * tile + lax.broadcasted_iota(jnp.int32, (tile, width), 0)
    down = jnp.where(weight_unit < hidden_units, down_ref[...].astype(jnp.float32), 0.0)
    terms = bdot(placed, down.astype(jnp.bfloat16))
    for b in range(count):
        piece = terms[:, b * half : (b + 1) * half]
        for r in range(groups):
            part_buf[b, r] = piece[r : r + 1]

    def part_copy(k, slot, peer):
        return pltpu.make_async_remote_copy(
            src_ref=part_buf.at[lax.rem(peer, count), peer // count],
            dst_ref=take_buf.at[slot],
            send_sem=part_send.at[k],
            recv_sem=part_recv.at[slot],
            device_id=(peer // count, lax.rem(peer, count)),
            device_id_type=MESH,
        )

    @pl.loop(1, devices)
    def _(k):
        part_copy(k, me, lax.rem(me + k, devices)).start()

    take_buf[me] = part_buf[blk, grp]
    moved = bdot(picker, resid_f.astype(jnp.bfloat16))
    rows_ref[...] = moved
    own_row = own_part(rows_ref[pl.ds(grp, 1), :], blk, count)

    @pl.loop(1, devices)
    def _(k):
        peer = lax.rem(me + k, devices)
        part_copy(k, peer, peer).wait_recv()

    out_ref[...] = (own_row + jnp.sum(take_buf[...], axis=0)).astype(jnp.bfloat16)

    @pl.loop(1, groups)
    def _(k):
        row_copy(k, grp, lax.rem(grp + k, groups)).wait_send()

    @pl.loop(1, devices)
    def _(k):
        part_copy(k, me, lax.rem(me + k, devices)).wait_send()


def ffn_spread(resid, ffn_gain, slot_request, w_gate_up, w_down):
    groups = lax.axis_size("req")
    count = lax.axis_size("blk")
    width = resid.shape[1]
    units = w_down.shape[0]
    tile = -(-units // (groups * 128)) * 128
    last = -(-units // tile) - 1
    vmem = pl.BlockSpec(memory_space=pltpu.VMEM)
    return pl.pallas_call(
        partial(ffn_kernel, groups, count, tile, units),
        grid=(1,),
        out_shape=jax.ShapeDtypeStruct((1, width // count), jnp.bfloat16),
        in_specs=[
            vmem,
            vmem,
            pl.BlockSpec(memory_space=pltpu.SMEM),
            pl.BlockSpec(
                (2, width, tile), lambda i: (0, 0, jnp.minimum(lax.axis_index("req"), last))
            ),
            pl.BlockSpec((tile, width), lambda i: (jnp.minimum(lax.axis_index("req"), last), 0)),
        ],
        out_specs=vmem,
        scratch_shapes=[
            pltpu.VMEM((groups, 1, width), jnp.float32),
            pltpu.VMEM((groups, width), jnp.float32),
            pltpu.VMEM((count, groups, 1, width // count), jnp.float32),
            pltpu.VMEM((groups * count, 1, width // count), jnp.float32),
            pltpu.SemaphoreType.DMA((groups,)),
            pltpu.SemaphoreType.DMA((groups,)),
            pltpu.SemaphoreType.DMA((groups * count,)),
            pltpu.SemaphoreType.DMA((groups * count,)),
        ],
        compiler_params=pltpu.CompilerParams(
            collective_id=1, has_side_effects=True, vmem_limit_bytes=VMEM_BYTES
        ),
    )(resid, ffn_gain, slot_request, w_gate_up, w_down)


def ffn_plain(resid, ffn_gain, slot_request, w_gate_up, w_down):
    blk_index = lax.axis_index("blk")
    grp_index = lax.axis_index("req")
    resid_f = resid.astype(jnp.float32)
    ffn_in = (resid_f * rms_scale(resid_f) * ffn_gain).astype(jnp.bfloat16)
    ffn_hidden = (silu(bdot(ffn_in, w_gate_up[0])) * bdot(ffn_in, w_gate_up[1])).astype(
        jnp.bfloat16
    )
    ffn_out = lax.psum(bdot(ffn_hidden, w_down), "blk")
    final_rows = (resid_f + ffn_out).astype(jnp.bfloat16)
    every_row = lax.all_gather(final_rows, "req", axis=0, tiled=True)
    part = resid.shape[1] // lax.axis_size("blk")
    columns = lax.dynamic_slice_in_dim(every_row, blk_index * part, part, 1)
    picker = (slot_request[None, :] == grp_index).astype(jnp.bfloat16)
    return bdot(picker, columns).astype(jnp.bfloat16)


def per_device(
    hidden,
    slot_request,
    cache_length,
    block_keep,
    stored_keys,
    stored_values,
    ssm_state,
    norm_gain,
    query_key_value_weight,
    w_attn_out,
    mamba_in,
    select_proj,
    step_proj,
    step_bias,
    decay_log,
    skip_gain,
    w_mamba_out,
    ffn_gain,
    w_gate_up,
    w_down,
):
    resid, fresh_entry, new_state = mix_branches(
        hidden, cache_length, block_keep, stored_keys, stored_values, ssm_state, norm_gain,
        query_key_value_weight, w_attn_out, mamba_in, select_proj, step_proj, step_bias,
        decay_log, skip_gain, w_mamba_out,
    )
    ffn = ffn_spread if lax.axis_size("req") <= 16 else ffn_plain
    hidden_out = ffn(resid, ffn_gain, slot_request, w_gate_up, w_down)
    return (hidden_out, fresh_entry, new_state)


def solution(mesh):
    return jax.shard_map(
        per_device,
        mesh=mesh,
        in_specs=(
            P("req", None),
            P(),
            P("req"),
            P("req", "blk"),
            P("req", "blk", None),
            P("req", "blk", None),
            P("req", None, "blk"),
            P(),
            P("blk", None),
            P("blk", None),
            P(None, None, "blk"),
            P("blk", None),
            P(None, "blk"),
            P("blk"),
            P(None, "blk"),
            P("blk"),
            P("blk", None),
            P(),
            P(None, None, "blk"),
            P("blk", None),
        ),
        out_specs=(P("req", "blk"), P("req", None), P("req", None, "blk")),
        check_vma=False,
    )
```

time: 103 us -> 56.8 us (0.55)
  blocking collectives: 58.2 us -> 0 us
  Pallas kernels: 0 us -> 33.2 us
  matrix products: 29.2 us -> 0 us
  local copies, waits for them, and re-layouts: 6.05 us -> 21.7 us
  other arithmetic: 6.16 us -> 0 us
  between operations: 3.02 us -> 1.3 us
    all_gather x4 -> x0, blocking collectives: 48.1 us -> none  [the longest x1 42.7 us: per_device(): every_row = lax.all_gather(final_rows, 'req', axis=0, tiled=True)]
    pallas_call x0 -> x2, Pallas kernels: none -> 33.2 us  [the longest x1 21 us: ffn_spread(): pl.pallas_call(partial(ffn_kernel, groups, count, tile, units), grid=(1,)...]
    dot_general x14 -> x0, matrix products: 29.2 us -> none  [the longest x1 5 us: per_device(): gate = jnp.dot(ffn_in, w_gate_up[0], preferred_element_type=jnp.float32)]
    unnamed x26 -> x11, local copies, waits for them, and re-layouts: 1.4 us -> 21.7 us
    psum x3 -> x0, blocking collectives: 10.1 us -> none  [the longest x1 5.11 us: per_device(): qkv_full, select_full = lax.psum((qkv_part, select_part), 'blk')]
    reduce_sum x5 -> x0, other arithmetic: 3.06 us -> none  [the longest x2 2.1 us: rms_scale(): jnp.mean(block_values * block_values, axis=-1, keepdims=True) + epsilon]
    slice x4 -> x0, local copies, waits for them, and re-layouts: 2.87 us -> none  [the longest x1 1.32 us: per_device(): fresh_entry = qkv_bf[:, att_width:]]
    mul x3 -> x0, other arithmetic: 1.41 us -> none  [the longest x1 0.72 us: per_device(): step_size * inner_f]
where the time goes in v1:
time: 56.8 us; the launch traced here: 56.2 us
  Pallas kernels  33.2 us (58%)
  local copies, waits for them, and re-layouts  21.7 us (38%)
  between operations  1.3 us (2%)
    unnamed x11, local copies, waits for them, and re-layouts  21.7 us
    pallas_call x1, Pallas kernels, ffn_spread(): pl.pallas_call(partial(ffn_kernel, groups, count, tile, units), grid=(1,)...  21 us
    pallas_call x1, Pallas kernels, mix_branches(): pl.pallas_call(partial(branch_kernel, count), out_shape=(jax.ShapeDtypeSt...  12.1 us

profile of v1, /device:TPU:0, one launch (start us, length us, event | category | flops | bytes accessed | tf_op | source)
XLA Modules:
  0.0 56.2 jit_solution(13909914091442194038)
XLA Ops:
  1.3 2.3 %copy.23.keys_hbm = bf16[1,1024,320]{2,1,0:T(8,128)(2,1)} copy(bf16[1,1024,320]{1,2,0:T(8,128)(2,1)} %param.24) | data formatting | bytes 1310720 | tf_op args[4]
  3.5 2.3 %copy.24.values_hbm = bf16[1,1024,320]{2,1,0:T(8,128)(2,1)} copy(bf16[1,1024,320]{1,2,0:T(8,128)(2,1)} %param.25) | data formatting | bytes 1310720 | tf_op args[5]
  5.8 2.2 %copy.25.select_hbm = bf16[1600,132]{1,0:T(8,128)(2,1)} copy(bf16[1600,132]{0,1:T(8,128)(2,1)} %param.31) | data formatting | bytes 844800 | tf_op args[11]
  8.0 12.1 %shard_map.211 = (bf16[1,1600]{1,0:T(2,128)(2,1)}, bf16[1,640]{1,0:T(2,128)(2,1)}, f32[1,16,1600]{2,1,0:T(8,128)}) custom-call(bf16[1,1600]{1,0:T(2,128)(2,1)} %hidden_ref.1, s32[1]{0:T(128)S(6)} %copy.30.length_ref, s32[1,8]{1,0:T(1,128)} %keep_ref.1, f32[1,16,1600]{2,1,0:T(8,128)} %state_ref.1, f32[1600]{0:T(1024)} %norm_ref.1, f32[1600]{0:T(1024)} %bias_ref.1, ...), custom_call_target="tpu_custom_call" | custom-call | tf_op jit(solution)/shard_map/pallas_call | solution.py:326
  20.1 12.5 %copy.26.down_ref = bf16[2752,1600]{1,0:T(8,128)(2,1)} copy(bf16[2752,1600]{0,1:T(8,128)(2,1)} %param.39) | data formatting | bytes 17612800 | tf_op args[19]
  32.6 0.0 copy-start.1
  32.6 0.0 copy-start
  32.7 21.0 %shard_map.212 = bf16[1,800]{1,0:T(2,128)(2,1)} custom-call(bf16[1,1600]{1,0:T(2,128)(2,1)} %get-tuple-element.6.resid_ref, f32[1600]{0:T(1024)} %gain_ref.1, s32[16]{0:T(128)} %slot_ref.1, bf16[2,1600,2752]{2,1,0:T(8,128)(2,1)} %gate_up_ref.1, bf16[2752,1600]{1,0:T(8,128)(2,1)} %copy.26.down_ref), custom_call_target="tpu_custom_call" | custom-call | tf_op jit(solution)/shard_map/pallas_call | solution.py:471
  53.7 1.3 %copy.31 = bf16[1,800]{1,0:T(2,128)(2,1)} copy(bf16[1,800]{1,0:T(2,128)(2,1)} %shard_map.212) | data formatting | bytes 3200
  55.0 0.0 copy-done.1
  55.0 0.6 %copy.32 = bf16[1,640]{1,0:T(2,128)(2,1)} copy(bf16[1,640]{1,0:T(2,128)(2,1)S(1)} %copy-done.1) | data formatting | bytes 2560
  55.5 0.0 copy-done
  55.5 0.6 %copy.33 = f32[1,16,1600]{2,1,0:T(8,128)} copy(f32[1,16,1600]{2,1,0:T(8,128)S(1)} %copy-done) | data formatting | bytes 204800
Async XLA Ops:
  32.6 22.3 %copy-start.1 = (bf16[1,640]{1,0:T(2,128)(2,1)S(1)}, bf16[1,640]{1,0:T(2,128)(2,1)}, u32[]{:S(2)}) copy-start(bf16[1,640]{1,0:T(2,128)(2,1)} %get-tuple-element.13) | copy-start | bytes 3844
  32.6 22.9 %copy-start = (f32[1,16,1600]{2,1,0:T(8,128)S(1)}, f32[1,16,1600]{2,1,0:T(8,128)}, u32[]{:S(2)}) copy-start(f32[1,16,1600]{2,1,0:T(8,128)} %get-tuple-element.14) | copy-start | bytes 307204

commit v2 on v1

--- a/solution.py
+++ b/solution.py
@@ -35,6 +35,12 @@
 
 def bdot(left, right):
     return jnp.dot(left, right, preferred_element_type=jnp.float32)
+
+
+def bdot_t(left, right):
+    return lax.dot_general(
+        left, right, (((1,), (1,)), ((), ())), preferred_element_type=jnp.float32
+    )
 
 
 def row_dot(row, weight):
@@ -138,7 +144,7 @@
     me = lax.axis_index("blk")
     width = hidden_ref.shape[1]
     channels = state_ref.shape[2]
-    positions = keys_ref.shape[0]
+    positions = keys_ref.shape[1]
     key_width = KEY_HEADS * HEAD_SIZE
     group = QUERY_HEADS // KEY_HEADS
     att_width = QUERY_HEADS * HEAD_SIZE
@@ -188,7 +194,7 @@
     inner_act = silu(feature_dot(0, load_x)).astype(jnp.bfloat16)
     inner_f = inner_act.astype(jnp.float32)
     load_select.wait()
-    sel_buf[me] = row_dot(inner_act, select_w[...])
+    sel_buf[me] = bdot_t(jnp.broadcast_to(inner_act, (ROWS, channels)), select_w[...])[0:1]
     sent_sel = send_all(sel_buf, send_sem, recv_sem, 1, count)
 
     wait_all(sent_qkv, qkv_buf, send_sem, recv_sem, 0, count)
@@ -215,12 +221,7 @@
 
     scale = HEAD_SIZE ** (-0.5)
     load_keys.wait()
-    scores = (
-        lax.dot_general(
-            query_bf, keys_ref[...], (((1,), (1,)), ((), ())), preferred_element_type=jnp.float32
-        )
-        * scale
-    )
+    scores = bdot(query_bf, keys_ref[...]) * scale
     lane = lax.broadcasted_iota(jnp.int32, (1, positions), 1)
     kept = jnp.zeros((1, positions), jnp.int32)
     for j in range(positions // BLOCK_POSITIONS):
@@ -233,7 +234,7 @@
     weights = jnp.where(live, jnp.exp(masked - local_max), 0.0)
     local_sum = jnp.sum(weights, axis=-1, keepdims=True)
     load_values.wait()
-    stat_buf[me, :, :key_width] = bdot(weights.astype(jnp.bfloat16), values_ref[...])
+    stat_buf[me, :, :key_width] = bdot_t(weights.astype(jnp.bfloat16), values_ref[...])
     stat_lane = lax.broadcasted_iota(jnp.int32, (HEAD_ROWS, 128), 1)
     stat_buf[me, :, STAT_LANES - 128 :] = jnp.where(stat_lane < 64, local_max, local_sum)
     sent_stat = send_all(stat_buf, send_sem, recv_sem, 2, count)
@@ -322,6 +323,9 @@
     vmem = pl.BlockSpec(memory_space=pltpu.VMEM)
     smem = pl.BlockSpec(memory_space=pltpu.SMEM)
     hbm = pl.BlockSpec(memory_space=pl.ANY)
+    stored_keys, stored_values, select_proj = (
+        jnp.swapaxes(a, -1, -2) for a in (stored_keys, stored_values, select_proj)
+    )
     big = (query_key_value_weight, w_attn_out, mamba_in, select_proj, step_proj, w_mamba_out)
     return pl.pallas_call(
         partial(branch_kernel, count),
@@ -339,7 +343,7 @@
         + [pltpu.VMEM(w.shape, w.dtype) for w in big]
         + [
             pltpu.VMEM((count, 1, qkv_width), jnp.float32),
-            pltpu.VMEM((count, 1, select_proj.shape[1]), jnp.float32),
+            pltpu.VMEM((count, 1, select_proj.shape[0]), jnp.float32),
             pltpu.VMEM((count, HEAD_ROWS, STAT_LANES), jnp.float32),
             pltpu.VMEM((count, 1, width), jnp.float32),
             pltpu.SemaphoreType.DMA((32,)),
@@ -417,9 +421,9 @@
     request = lax.broadcasted_iota(jnp.int32, (groups, groups), 0)
     picker = (slots == request).astype(jnp.float32).astype(jnp.bfloat16)
     placed = bdot(picker, ffn_hidden).astype(jnp.bfloat16)
-    weight_unit = grp * tile + lax.broadcasted_iota(jnp.int32, (tile, width), 0)
+    weight_unit = grp * tile + lax.broadcasted_iota(jnp.int32, (width, tile), 1)
     down = jnp.where(weight_unit < hidden_units, down_ref[...].astype(jnp.float32), 0.0)
-    terms = bdot(placed, down.astype(jnp.bfloat16))
+    terms = bdot_t(placed, down.astype(jnp.bfloat16))
     for b in range(count):
         piece = terms[:, b * half : (b + 1) * half]
         for r in range(groups):
@@ -479,7 +483,7 @@
             pl.BlockSpec(
                 (2, width, tile), lambda i: (0, 0, jnp.minimum(lax.axis_index("req"), last))
             ),
-            pl.BlockSpec((tile, width), lambda i: (jnp.minimum(lax.axis_index("req"), last), 0)),
+            pl.BlockSpec((width, tile), lambda i: (0, jnp.minimum(lax.axis_index("req"), last))),
         ],
         out_specs=vmem,
         scratch_shapes=[
@@ -495,7 +499,7 @@
         compiler_params=pltpu.CompilerParams(
             collective_id=1, has_side_effects=True, vmem_limit_bytes=VMEM_BYTES
         ),
-    )(resid, ffn_gain, slot_request, w_gate_up, w_down)
+    )(resid, ffn_gain, slot_request, w_gate_up, w_down.T)
 
 
 def ffn_plain(resid, ffn_gain, slot_request, w_gate_up, w_down):

time: 56.8 us -> 37.3 us (0.66)
  local copies, waits for them, and re-layouts: 21.7 us -> 2.49 us
    unnamed x11 -> x7, local copies, waits for them, and re-layouts: 21.7 us -> 2.49 us
where the time goes in v2:
time: 37.3 us; the launch traced here: 37.1 us
  Pallas kernels  33.3 us (89%)
  local copies, waits for them, and re-layouts  2.49 us (7%)
  between operations  1.32 us (4%)
    pallas_call x1, Pallas kernels, ffn_spread(): pl.pallas_call(partial(ffn_kernel, groups, count, tile, units), grid=(1,)...  21.2 us
    pallas_call x1, Pallas kernels, mix_branches(): pl.pallas_call(partial(branch_kernel, count), out_shape=(jax.ShapeDtypeSt...  12.1 us
    unnamed x7, local copies, waits for them, and re-layouts  2.49 us

profile of v2, /device:TPU:0, one launch (start us, length us, event | category | flops | bytes accessed | tf_op | source)
XLA Modules:
  0.0 37.1 jit_solution(9552251108207603809)
XLA Ops:
  1.3 12.1 %shard_map.211 = (bf16[1,1600]{1,0:T(2,128)(2,1)}, bf16[1,640]{1,0:T(2,128)(2,1)}, f32[1,16,1600]{2,1,0:T(8,128)}) custom-call(bf16[1,1600]{1,0:T(2,128)(2,1)} %hidden_ref.1, s32[1]{0:T(128)S(6)} %copy.26.length_ref, s32[1,8]{1,0:T(1,128)} %keep_ref.1, f32[1,16,1600]{2,1,0:T(8,128)} %state_ref.1, f32[1600]{0:T(1024)} %norm_ref.1, f32[1600]{0:T(1024)} %bias_ref.1, ...), custom_call_target="tpu_custom_call" | custom-call | tf_op jit(solution)/shard_map/pallas_call | solution.py:330
  13.4 0.0 copy-start.1
  13.4 0.0 copy-start
  13.4 21.2 %shard_map.212 = bf16[1,800]{1,0:T(2,128)(2,1)} custom-call(bf16[1,1600]{1,0:T(2,128)(2,1)} %get-tuple-element.6.resid_ref, f32[1600]{0:T(1024)} %gain_ref.1, s32[16]{0:T(128)} %slot_ref.1, bf16[2,1600,2752]{2,1,0:T(8,128)(2,1)} %gate_up_ref.1, bf16[1600,2752]{1,0:T(8,128)(2,1)} %bitcast.4), custom_call_target="tpu_custom_call" | custom-call | tf_op jit(solution)/shard_map/pallas_call | solution.py:475
  34.6 1.3 %copy.27 = bf16[1,800]{1,0:T(2,128)(2,1)} copy(bf16[1,800]{1,0:T(2,128)(2,1)} %shard_map.212) | data formatting | bytes 3200
  35.9 0.0 copy-done.1
  35.9 0.6 %copy.28 = bf16[1,640]{1,0:T(2,128)(2,1)} copy(bf16[1,640]{1,0:T(2,128)(2,1)S(1)} %copy-done.1) | data formatting | bytes 2560
  36.5 0.0 copy-done
  36.5 0.6 %copy.29 = f32[1,16,1600]{2,1,0:T(8,128)} copy(f32[1,16,1600]{2,1,0:T(8,128)S(1)} %copy-done) | data formatting | bytes 204800
Async XLA Ops:
  13.4 22.5 %copy-start.1 = (bf16[1,640]{1,0:T(2,128)(2,1)S(1)}, bf16[1,640]{1,0:T(2,128)(2,1)}, u32[]{:S(2)}) copy-start(bf16[1,640]{1,0:T(2,128)(2,1)} %get-tuple-element.13) | copy-start | bytes 3844
  13.4 23.0 %copy-start = (f32[1,16,1600]{2,1,0:T(8,128)S(1)}, f32[1,16,1600]{2,1,0:T(8,128)}, u32[]{:S(2)}) copy-start(f32[1,16,1600]{2,1,0:T(8,128)} %get-tuple-element.14) | copy-start | bytes 307204

commit v3 on v2

--- a/solution.py
+++ b/solution.py
@@ -23,6 +23,7 @@
 ROWS = 16
 HEAD_ROWS = 32
 STAT_LANES = 512
+LANES = 128
 
 
 def rms_scale(block_values):
@@ -104,43 +105,31 @@
     return result
 
 
-def branch_kernel(
+def layer_kernel(
     count,
-    hidden_ref,
-    length_ref,
-    keep_ref,
-    state_ref,
-    norm_ref,
-    bias_ref,
-    decay_ref,
-    skip_ref,
-    keys_hbm,
-    values_hbm,
-    qkv_hbm,
-    attn_hbm,
-    mamba_hbm,
-    select_hbm,
-    step_hbm,
-    out_hbm,
-    resid_ref,
-    fresh_ref,
-    new_state_ref,
-    keys_ref,
-    values_ref,
-    qkv_w,
-    attn_w,
-    mamba_w,
-    select_w,
-    step_w,
-    out_w,
-    qkv_buf,
-    sel_buf,
-    stat_buf,
-    mix_buf,
-    load_sem,
-    send_sem,
-    recv_sem,
+    groups,
+    tile,
+    spread_ffn,
+    *refs,
 ):
+    (
+        hidden_ref, length_ref, keep_ref, state_ref, norm_ref, bias_ref, decay_ref, skip_ref,
+        keys_hbm, values_hbm, qkv_hbm, attn_hbm, mamba_hbm, select_hbm, step_hbm, out_hbm,
+    ) = refs[:16]
+    refs = refs[16:]
+    if spread_ffn:
+        gain_ref, slot_ref, gate_up_hbm, down_hbm = refs[:4]
+        refs = refs[4:]
+    resid_ref, fresh_ref, new_state_ref = refs[:3]
+    (
+        keys_ref, values_ref, qkv_w, attn_w, mamba_w, select_w, step_w, out_w,
+        qkv_buf, sel_buf, stat_buf, mix_buf, load_sem, send_sem, recv_sem,
+    ) = refs[3:18]
+    if spread_ffn:
+        (
+            gate_up_w, down_w, gate_up_tail, down_tail, row_buf, rows_ref, part_buf, take_buf,
+            far_send, far_recv,
+        ) = refs[18:]
     me = lax.axis_index("blk")
     width = hidden_ref.shape[1]
     channels = state_ref.shape[2]
@@ -168,12 +157,74 @@
     load_out = [load(out_hbm.at[a:b], out_w.at[a:b]) for a, b in chan_cuts]
     load_attn = load(attn_hbm, attn_w)
 
+    if spread_ffn:
+        grp = lax.axis_index("req")
+        units = down_hbm.shape[1]
+        last = -(-units // tile) - 1
+        place = jnp.minimum(grp, last)
+        ffn_loads = []
+        for p in range(tile // LANES):
+            avail = min(LANES, units - last * tile - p * LANES)
+            window = pl.ds(pl.multiple_of(place * tile + p * LANES, LANES), LANES)
+            piece = slice(p * LANES, (p + 1) * LANES)
+            first = 24 + 4 * p
+            full = [
+                pltpu.make_async_copy(
+                    gate_up_hbm.at[:, :, window], gate_up_w.at[:, :, piece], load_sem.at[first]
+                ),
+                pltpu.make_async_copy(
+                    down_hbm.at[:, window], down_w.at[:, piece], load_sem.at[first + 1]
+                ),
+            ]
+            tail = []
+            if 0 < avail < LANES:
+                end = slice(units - avail, units)
+                tail = [
+                    pltpu.make_async_copy(
+                        gate_up_hbm.at[:, :, end], gate_up_tail, load_sem.at[first + 2]
+                    ),
+                    pltpu.make_async_copy(down_hbm.at[:, end], down_tail, load_sem.at[first + 3]),
+                ]
+            ffn_loads.append((avail, piece, full, tail))
+
+        def each_load(act):
+            for avail, piece, full, tail in ffn_loads:
+                if avail == LANES:
+                    for copy in full:
+                        act(copy)
+                    continue
+
+                @pl.when(grp < last)
+                def _():
+                    for copy in full:
+                        act(copy)
+
+                if tail:
+
+                    @pl.when(grp >= last)
+                    def _():
+                        for copy in tail:
+                            act(copy)
+
+        each_load(lambda copy: copy.start())
+
     barrier = pltpu.get_barrier_semaphore()
     for k in range(1, count):
         pl.semaphore_signal(
             barrier, inc=1, device_id={"blk": lax.rem(me + k, count)}, device_id_type=MESH
         )
-    pl.semaphore_wait(barrier, count - 1)
+    if spread_ffn:
+
+        @pl.loop(1, groups)
+        def _(k):
+            for b in range(count):
+                pl.semaphore_signal(
+                    barrier, inc=1, device_id=(lax.rem(grp + k, groups), b), device_id_type=MESH
+                )
+
+        pl.semaphore_wait(barrier, groups * count - 1)
+    else:
+        pl.semaphore_wait(barrier, count - 1)
 
     hidden_f = hidden_ref[...].astype(jnp.float32)
     normed_f = hidden_f * rms_scale(hidden_f) * norm_ref[...].reshape(1, width)
@@ -308,13 +359,102 @@
     mix_buf[me] = 0.5 * mix
     sent_mix = send_all(mix_buf, send_sem, recv_sem, 3, count)
     wait_all(sent_mix, mix_buf, send_sem, recv_sem, 3, count)
-    resid_ref[...] = (hidden_f + total_of(mix_buf, count)).astype(jnp.bfloat16)
-
-
-def mix_branches(
+    resid = (hidden_f + total_of(mix_buf, count)).astype(jnp.bfloat16)
+    if not spread_ffn:
+        resid_ref[...] = resid
+        return
+
+    row_buf[grp] = resid.astype(jnp.float32)
+
+    @pl.loop(1, groups)
+    def _(k):
+        pltpu.make_async_remote_copy(
+            src_ref=row_buf.at[grp],
+            dst_ref=row_buf.at[grp],
+            send_sem=far_send.at[0],
+            recv_sem=far_recv.at[0],
+            device_id=(lax.rem(grp + k, groups), me),
+            device_id_type=MESH,
+        ).start()
+
+    lane = lax.broadcasted_iota(jnp.int32, (groups, groups), 1)
+    slots = jnp.zeros((groups, groups), jnp.int32)
+    for s in range(groups):
+        slots = jnp.where(lane == s, slot_ref[s], slots)
+    request = lax.broadcasted_iota(jnp.int32, (groups, groups), 0)
+    picker = (slots == request).astype(jnp.float32).astype(jnp.bfloat16)
+    each_load(lambda copy: copy.wait())
+    for avail, piece, _, tail in ffn_loads:
+        if avail == LANES:
+            continue
+
+        @pl.when(grp >= last)
+        def _():
+            gate_up_w[:, :, piece] = jnp.zeros_like(gate_up_w[:, :, piece])
+            down_w[:, piece] = jnp.zeros_like(down_w[:, piece])
+            if tail:
+                begin = piece.start
+                gate_up_w[:, :, begin : begin + avail] = gate_up_tail[...]
+                down_w[:, begin : begin + avail] = down_tail[...]
+
+    def far_wait(stage, buf, amount):
+        return pltpu.make_async_remote_copy(
+            src_ref=buf.at[pl.ds(0, amount)],
+            dst_ref=buf.at[pl.ds(0, amount)],
+            send_sem=far_send.at[stage],
+            recv_sem=far_recv.at[stage],
+            device_id=(lax.rem(grp + 1, groups), me),
+            device_id_type=MESH,
+        )
+
+    far_wait(0, row_buf, groups - 1).wait_recv()
+    for r in range(groups):
+        rows_ref[r : r + 1, :] = row_buf[r]
+    resid_f = rows_ref[...]
+    ffn_in = (resid_f * rms_scale(resid_f) * gain_ref[...].reshape(1, width)).astype(jnp.bfloat16)
+    unit = grp * tile + lax.broadcasted_iota(jnp.int32, (groups, tile), 1)
+    ffn_hidden = silu(bdot(ffn_in, gate_up_w[0])) * bdot(ffn_in, gate_up_w[1])
+    ffn_hidden = jnp.where(unit < units, ffn_hidden, 0.0).astype(jnp.bfloat16)
+    placed = bdot(picker, ffn_hidden).astype(jnp.bfloat16)
+    terms = bdot_t(placed, down_w[...])
+    half = width // count
+    for b in range(count):
+        piece = terms[:, b * half : (b + 1) * half]
+        for r in range(groups):
+            part_buf[b, r] = piece[r : r + 1]
+    slot = grp * count + me
+
+    def part_send(peer, blk):
+        pltpu.make_async_remote_copy(
+            src_ref=part_buf.at[blk, peer],
+            dst_ref=take_buf.at[slot],
+            send_sem=far_send.at[1],
+            recv_sem=far_recv.at[1],
+            device_id=(peer, blk),
+            device_id_type=MESH,
+        ).start()
+
+    @pl.loop(1, groups)
+    def _(k):
+        for b in range(count):
+            part_send(lax.rem(grp + k, groups), b)
+
+    for k in range(1, count):
+        part_send(grp, lax.rem(me + k, count))
+    take_buf[slot] = part_buf[me, grp]
+    rows_ref[...] = bdot(picker, resid_f.astype(jnp.bfloat16))
+    own_row = own_part(rows_ref[pl.ds(grp, 1), :], me, count)
+    amount = groups * count - 1
+    far_wait(1, take_buf, amount).wait_recv()
+    resid_ref[...] = (own_row + jnp.sum(take_buf[...], axis=0)).astype(jnp.bfloat16)
+    far_wait(0, row_buf, groups - 1).wait_send()
+    far_wait(1, take_buf, amount).wait_send()
+
+
+def layer(
     hidden, cache_length, block_keep, stored_keys, stored_values, ssm_state, norm_gain,
     query_key_value_weight, w_attn_out, mamba_in, select_proj, step_proj, step_bias, decay_log,
-    skip_gain, w_mamba_out,
+    skip_gain, w_mamba_out, ffn_gain, slot_request, w_gate_up, w_down, spread_ffn,
 ):
     count = lax.axis_size("blk")
     width = hidden.shape[1]
@@ -327,14 +467,35 @@
         jnp.swapaxes(a, -1, -2) for a in (stored_keys, stored_values, select_proj)
     )
     big = (query_key_value_weight, w_attn_out, mamba_in, select_proj, step_proj, w_mamba_out)
+    groups = lax.axis_size("req")
+    units = w_down.shape[0]
+    tile = -(-units // (groups * LANES)) * LANES
+    ffn_args, ffn_specs, ffn_scratch = [], [], []
+    if spread_ffn:
+        tail = units % LANES or LANES
+        half = width // count
+        ffn_args = [ffn_gain, slot_request, w_gate_up, w_down.T]
+        ffn_specs = [vmem, smem, hbm, hbm]
+        ffn_scratch = [
+            pltpu.VMEM((2, width, tile), jnp.bfloat16),
+            pltpu.VMEM((width, tile), jnp.bfloat16),
+            pltpu.VMEM((2, width, tail), jnp.bfloat16),
+            pltpu.VMEM((width, tail), jnp.bfloat16),
+            pltpu.VMEM((groups, 1, width), jnp.float32),
+            pltpu.VMEM((groups, width), jnp.float32),
+            pltpu.VMEM((count, groups, 1, half), jnp.float32),
+            pltpu.VMEM((groups * count, 1, half), jnp.float32),
+            pltpu.SemaphoreType.DMA((2,)),
+            pltpu.SemaphoreType.DMA((2,)),
+        ]
     return pl.pallas_call(
-        partial(branch_kernel, count),
+        partial(layer_kernel, count, groups, tile, spread_ffn),
         out_shape=(
-            jax.ShapeDtypeStruct(hidden.shape, jnp.bfloat16),
+            jax.ShapeDtypeStruct((1, width // count if spread_ffn else width), jnp.bfloat16),
             jax.ShapeDtypeStruct((1, 2 * KEY_HEADS * HEAD_SIZE), jnp.bfloat16),
             jax.ShapeDtypeStruct(ssm_state.shape, jnp.float32),
         ),
-        in_specs=[vmem, smem, smem, vmem, vmem, vmem, vmem, vmem] + [hbm] * 8,
+        in_specs=[vmem, smem, smem, vmem, vmem, vmem, vmem, vmem] + [hbm] * 8 + ffn_specs,
         out_specs=(vmem, vmem, vmem),
         scratch_shapes=[
             pltpu.VMEM(stored_keys.shape[1:], jnp.bfloat16),
@@ -346,160 +507,18 @@
             pltpu.VMEM((count, 1, select_proj.shape[0]), jnp.float32),
             pltpu.VMEM((count, HEAD_ROWS, STAT_LANES), jnp.float32),
             pltpu.VMEM((count, 1, width), jnp.float32),
-            pltpu.SemaphoreType.DMA((32,)),
+            pltpu.SemaphoreType.DMA((40,)),
             pltpu.SemaphoreType.DMA((4, count)),
             pltpu.SemaphoreType.DMA((4, count)),
-        ],
+        ]
+        + ffn_scratch,
         compiler_params=pltpu.CompilerParams(
             collective_id=0, has_side_effects=True, vmem_limit_bytes=VMEM_BYTES
         ),
     )(
         hidden, cache_length, block_keep, ssm_state, norm_gain, step_bias, decay_log, skip_gain,
-        stored_keys, stored_values, *big,
-    )
-
-
-def ffn_kernel(
-    groups, count, tile, hidden_units,
-    resid_ref, gain_ref, slot_ref, gate_up_ref, down_ref,
-    out_ref,
-    row_buf, rows_ref, part_buf, take_buf, row_send, row_recv, part_send, part_recv,
-):
-    devices = groups * count
-    grp = lax.axis_index("req")
-    blk = lax.axis_index("blk")
-    me = grp * count + blk
-    width = resid_ref.shape[1]
-    half = width // count
-
-    barrier = pltpu.get_barrier_semaphore()
-
-    @pl.loop(1, devices)
-    def _(k):
-        target = lax.rem(me + k, devices)
-        pl.semaphore_signal(
-            barrier,
-            inc=1,
-            device_id=(target // count, lax.rem(target, count)),
-            device_id_type=MESH,
-        )
-
-    row_buf[grp] = resid_ref[...].astype(jnp.float32)
-    pl.semaphore_wait(barrier, devices - 1)
-
-    def row_copy(k, slot, peer):
-        return pltpu.make_async_remote_copy(
-            src_ref=row_buf.at[slot],
-            dst_ref=row_buf.at[slot],
-            send_sem=row_send.at[k],
-            recv_sem=row_recv.at[slot],
-            device_id=(peer, blk),
-            device_id_type=MESH,
-        )
-
-    @pl.loop(1, groups)
-    def _(k):
-        row_copy(k, grp, lax.rem(grp + k, groups)).start()
-
-    @pl.loop(1, groups)
-    def _(k):
-        peer = lax.rem(grp + k, groups)
-        row_copy(k, peer, peer).wait_recv()
-
-    for r in range(groups):
-        rows_ref[r : r + 1, :] = row_buf[r]
-    resid_f = rows_ref[...]
-    ffn_in = (resid_f * rms_scale(resid_f) * gain_ref[...].reshape(1, width)).astype(jnp.bfloat16)
-    gate = bdot(ffn_in, gate_up_ref[0])
-    upper = bdot(ffn_in, gate_up_ref[1])
-    unit = grp * tile + lax.broadcasted_iota(jnp.int32, (groups, tile), 1)
-    ffn_hidden = jnp.where(unit < hidden_units, silu(gate) * upper, 0.0).astype(jnp.bfloat16)
-    lane = lax.broadcasted_iota(jnp.int32, (groups, groups), 1)
-    slots = jnp.zeros((groups, groups), jnp.int32)
-    for s in range(groups):
-        slots = jnp.where(lane == s, slot_ref[s], slots)
-    request = lax.broadcasted_iota(jnp.int32, (groups, groups), 0)
-    picker = (slots == request).astype(jnp.float32).astype(jnp.bfloat16)
-    placed = bdot(picker, ffn_hidden).astype(jnp.bfloat16)
-    weight_unit = grp * tile + lax.broadcasted_iota(jnp.int32, (width, tile), 1)
-    down = jnp.where(weight_unit < hidden_units, down_ref[...].astype(jnp.float32), 0.0)
-    terms = bdot_t(placed, down.astype(jnp.bfloat16))
-    for b in range(count):
-        piece = terms[:, b * half : (b + 1) * half]
-        for r in range(groups):
-            part_buf[b, r] = piece[r : r + 1]
-
-    def part_copy(k, slot, peer):
-        return pltpu.make_async_remote_copy(
-            src_ref=part_buf.at[lax.rem(peer, count), peer // count],
-            dst_ref=take_buf.at[slot],
-            send_sem=part_send.at[k],
-            recv_sem=part_recv.at[slot],
-            device_id=(peer // count, lax.rem(peer, count)),
-            device_id_type=MESH,
-        )
-
-    @pl.loop(1, devices)
-    def _(k):
-        part_copy(k, me, lax.rem(me + k, devices)).start()
-
-    take_buf[me] = part_buf[blk, grp]
-    moved = bdot(picker, resid_f.astype(jnp.bfloat16))
-    rows_ref[...] = moved
-    own_row = own_part(rows_ref[pl.ds(grp, 1), :], blk, count)
-
-    @pl.loop(1, devices)
-    def _(k):
-        peer = lax.rem(me + k, devices)
-        part_copy(k, peer, peer).wait_recv()
-
-    out_ref[...] = (own_row + jnp.sum(take_buf[...], axis=0)).astype(jnp.bfloat16)
-
-    @pl.loop(1, groups)
-    def _(k):
-        row_copy(k, grp, lax.rem(grp + k, groups)).wait_send()
-
-    @pl.loop(1, devices)
-    def _(k):
-        part_copy(k, me, lax.rem(me + k, devices)).wait_send()
-
-
-def ffn_spread(resid, ffn_gain, slot_request, w_gate_up, w_down):
-    groups = lax.axis_size("req")
-    count = lax.axis_size("blk")
-    width = resid.shape[1]
-    units = w_down.shape[0]
-    tile = -(-units // (groups * 128)) * 128
-    last = -(-units // tile) - 1
-    vmem = pl.BlockSpec(memory_space=pltpu.VMEM)
-    return pl.pallas_call(
-        partial(ffn_kernel, groups, count, tile, units),
-        grid=(1,),
-        out_shape=jax.ShapeDtypeStruct((1, width // count), jnp.bfloat16),
-        in_specs=[
-            vmem,
-            vmem,
-            pl.BlockSpec(memory_space=pltpu.SMEM),
-            pl.BlockSpec(
-                (2, width, tile), lambda i: (0, 0, jnp.minimum(lax.axis_index("req"), last))
-            ),
-            pl.BlockSpec((width, tile), lambda i: (0, jnp.minimum(lax.axis_index("req"), last))),
-        ],
-        out_specs=vmem,
-        scratch_shapes=[
-            pltpu.VMEM((groups, 1, width), jnp.float32),
-            pltpu.VMEM((groups, width), jnp.float32),
-            pltpu.VMEM((count, groups, 1, width // count), jnp.float32),
-            pltpu.VMEM((groups * count, 1, width // count), jnp.float32),
-            pltpu.SemaphoreType.DMA((groups,)),
-            pltpu.SemaphoreType.DMA((groups,)),
-            pltpu.SemaphoreType.DMA((groups * count,)),
-            pltpu.SemaphoreType.DMA((groups * count,)),
-        ],
-        compiler_params=pltpu.CompilerParams(
-            collective_id=1, has_side_effects=True, vmem_limit_bytes=VMEM_BYTES
-        ),
-    )(resid, ffn_gain, slot_request, w_gate_up, w_down.T)
+        stored_keys, stored_values, *big, *ffn_args,
+    )
 
 
 def ffn_plain(resid, ffn_gain, slot_request, w_gate_up, w_down):
@@ -541,14 +560,15 @@
     w_gate_up,
     w_down,
 ):
-    resid, fresh_entry, new_state = mix_branches(
+    spread_ffn = lax.axis_size("req") <= 16
+    row, fresh_entry, new_state = layer(
         hidden, cache_length, block_keep, stored_keys, stored_values, ssm_state, norm_gain,
         query_key_value_weight, w_attn_out, mamba_in, select_proj, step_proj, step_bias,
-        decay_log, skip_gain, w_mamba_out,
-    )
-    ffn = ffn_spread if lax.axis_size("req") <= 16 else ffn_plain
-    hidden_out = ffn(resid, ffn_gain, slot_request, w_gate_up, w_down)
-    return (hidden_out, fresh_entry, new_state)
+        decay_log, skip_gain, w_mamba_out, ffn_gain, slot_request, w_gate_up, w_down, spread_ffn,
+    )
+    if not spread_ffn:
+        row = ffn_plain(row, ffn_gain, slot_request, w_gate_up, w_down)
+    return (row, fresh_entry, new_state)
 
 
 def solution(mesh):

time: 37.3 us -> 33.9 us (0.909)
  Pallas kernels: 33.3 us -> 28.3 us
  local copies, waits for them, and re-layouts: 2.49 us -> 4.06 us
    pallas_call x2 -> x1, Pallas kernels: 33.3 us -> 28.3 us  [layer(): pl.pallas_call(partial(layer_kernel, count, groups, tile, spread_ffn), ou...]
    unnamed x7 -> x3, local copies, waits for them, and re-layouts: 2.49 us -> 4.06 us
where the time goes in v3:
time: 33.9 us; the launch traced here: 33.6 us
  Pallas kernels  28.3 us (83%)
  local copies, waits for them, and re-layouts  4.06 us (12%)
  between operations  1.29 us (4%)
    pallas_call x1, Pallas kernels, layer(): pl.pallas_call(partial(layer_kernel, count, groups, tile, spread_ffn), ou...  28.3 us
    unnamed x3, local copies, waits for them, and re-layouts  4.06 us

profile of v3, /device:TPU:0, one launch (start us, length us, event | category | flops | bytes accessed | tf_op | source)
XLA Modules:
  0.0 33.6 jit_solution(14096730798394553907)
XLA Ops:
  1.3 28.3 %shard_map.211 = (bf16[1,800]{1,0:T(2,128)(2,1)}, bf16[1,640]{1,0:T(2,128)(2,1)}, f32[1,16,1600]{2,1,0:T(8,128)}) custom-call(bf16[1,1600]{1,0:T(2,128)(2,1)} %refs_0_.1, s32[1]{0:T(128)S(6)} %copy.26.refs_1_, s32[1,8]{1,0:T(1,128)} %refs_2_.1, f32[1,16,1600]{2,1,0:T(8,128)} %refs_3_.1, f32[1600]{0:T(1024)} %refs_4_.1, f32[1600]{0:T(1024)} %refs_5_.1, ...), custom_call_target="tpu_custom_call" | custom-call | tf_op jit(solution)/shard_map/pallas_call | solution.py:491
  29.6 1.3 %copy.27 = bf16[1,800]{1,0:T(2,128)(2,1)} copy(bf16[1,800]{1,0:T(2,128)(2,1)} %get-tuple-element.6) | data formatting | bytes 3200
  30.8 1.3 %copy.28 = bf16[1,640]{1,0:T(2,128)(2,1)} copy(bf16[1,640]{1,0:T(2,128)(2,1)} %get-tuple-element.7) | data formatting | bytes 2560
  32.1 1.5 %copy.29 = f32[1,16,1600]{2,1,0:T(8,128)} copy(f32[1,16,1600]{2,1,0:T(8,128)} %get-tuple-element.8) | data formatting | bytes 204800

commit v4 on v3

--- a/solution.py
+++ b/solution.py
@@ -364,7 +364,7 @@
         resid_ref[...] = resid
         return
 
-    row_buf[grp] = resid.astype(jnp.float32)
+    row_buf[grp] = resid
 
     @pl.loop(1, groups)
     def _(k):
@@ -409,20 +409,12 @@
 
     far_wait(0, row_buf, groups - 1).wait_recv()
     for r in range(groups):
-        rows_ref[r : r + 1, :] = row_buf[r]
+        rows_ref[r : r + 1, :] = row_buf[r].astype(jnp.float32)
     resid_f = rows_ref[...]
     ffn_in = (resid_f * rms_scale(resid_f) * gain_ref[...].reshape(1, width)).astype(jnp.bfloat16)
-    unit = grp * tile + lax.broadcasted_iota(jnp.int32, (groups, tile), 1)
-    ffn_hidden = silu(bdot(ffn_in, gate_up_w[0])) * bdot(ffn_in, gate_up_w[1])
-    ffn_hidden = jnp.where(unit < units, ffn_hidden, 0.0).astype(jnp.bfloat16)
-    placed = bdot(picker, ffn_hidden).astype(jnp.bfloat16)
-    terms = bdot_t(placed, down_w[...])
     half = width // count
-    for b in range(count):
-        piece = terms[:, b * half : (b + 1) * half]
-        for r in range(groups):
-            part_buf[b, r] = piece[r : r + 1]
     slot = grp * count + me
+    senders = (last + 1) * count
 
     def part_send(peer, blk):
         pltpu.make_async_remote_copy(
@@ -434,21 +426,63 @@
             device_id_type=MESH,
         ).start()
 
-    @pl.loop(1, groups)
-    def _(k):
+    @pl.when(grp <= last)
+    def _():
+        unit = grp * tile + lax.broadcasted_iota(jnp.int32, (groups, tile), 1)
+        ffn_hidden = silu(bdot(ffn_in, gate_up_w[0])) * bdot(ffn_in, gate_up_w[1])
+        ffn_hidden = jnp.where(unit < units, ffn_hidden, 0.0).astype(jnp.bfloat16)
+        placed = bdot(picker, ffn_hidden).astype(jnp.bfloat16)
+        terms = bdot_t(placed, down_w[...])
         for b in range(count):
-            part_send(lax.rem(grp + k, groups), b)
-
-    for k in range(1, count):
-        part_send(grp, lax.rem(me + k, count))
-    take_buf[slot] = part_buf[me, grp]
+            piece = terms[:, b * half : (b + 1) * half]
+            for r in range(groups):
+                part_buf[b, r] = piece[r : r + 1].astype(jnp.bfloat16)
+
+        @pl.loop(1, groups)
+        def _(k):
+            for b in range(count):
+                part_send(lax.rem(grp + k, groups), b)
+
+        for k in range(1, count):
+            part_send(grp, lax.rem(me + k, count))
+        take_buf[slot] = part_buf[me, grp]
+
     rows_ref[...] = bdot(picker, resid_f.astype(jnp.bfloat16))
     own_row = own_part(rows_ref[pl.ds(grp, 1), :], me, count)
-    amount = groups * count - 1
-    far_wait(1, take_buf, amount).wait_recv()
-    resid_ref[...] = (own_row + jnp.sum(take_buf[...], axis=0)).astype(jnp.bfloat16)
+
+    @pl.when(grp <= last)
+    def _():
+        far_wait(1, take_buf, senders - 1).wait_recv()
+
+    @pl.when(grp > last)
+    def _():
+        far_wait(1, take_buf, senders).wait_recv()
+
+    result = own_row
+    for k in range(senders):
+        result = result + take_buf[k].astype(jnp.float32)
+    resid_ref[...] = result.astype(jnp.bfloat16)
     far_wait(0, row_buf, groups - 1).wait_send()
-    far_wait(1, take_buf, amount).wait_send()
+
+    @pl.when(grp <= last)
+    def _():
+        far_wait(1, take_buf, groups * count - 1).wait_send()
+
+
+def hand_over_kernel(row_in, fresh_in, state_in, row_out, fresh_out, state_out):
+    row_out[...] = row_in[...]
+    fresh_out[...] = fresh_in[...]
+    state_out[...] = state_in[...]
+
+
+def hand_over(*results):
+    vmem = pl.BlockSpec(memory_space=pltpu.VMEM)
+    return pl.pallas_call(
+        hand_over_kernel,
+        out_shape=tuple(jax.ShapeDtypeStruct(r.shape, r.dtype) for r in results),
+        in_specs=[vmem] * 3,
+        out_specs=(vmem,) * 3,
+    )(*results)
 
 
 def layer(
@@ -481,10 +515,10 @@
             pltpu.VMEM((width, tile), jnp.bfloat16),
             pltpu.VMEM((2, width, tail), jnp.bfloat16),
             pltpu.VMEM((width, tail), jnp.bfloat16),
-            pltpu.VMEM((groups, 1, width), jnp.float32),
+            pltpu.VMEM((groups, 1, width), jnp.bfloat16),
             pltpu.VMEM((groups, width), jnp.float32),
-            pltpu.VMEM((count, groups, 1, half), jnp.float32),
-            pltpu.VMEM((groups * count, 1, half), jnp.float32),
+            pltpu.VMEM((count, groups, 1, half), jnp.bfloat16),
+            pltpu.VMEM((groups * count, 1, half), jnp.bfloat16),
             pltpu.SemaphoreType.DMA((2,)),
             pltpu.SemaphoreType.DMA((2,)),
         ]
@@ -568,7 +602,7 @@
     )
     if not spread_ffn:
         row = ffn_plain(row, ffn_gain, slot_request, w_gate_up, w_down)
-    return (row, fresh_entry, new_state)
+    return hand_over(row, fresh_entry, new_state)
 
 
 def solution(mesh):

time: 33.9 us -> 29.1 us (0.86)
  local copies, waits for them, and re-layouts: 4.06 us -> 0 us
  Pallas kernels: 28.3 us -> 27.6 us
    unnamed x3 -> x0, local copies, waits for them, and re-layouts: 4.06 us -> none
    pallas_call x1, Pallas kernels: 28.3 us -> 26.1 us  [layer(): pl.pallas_call(partial(layer_kernel, count, groups, tile, spread_ffn), ou...]
    pallas_call x0 -> x1, Pallas kernels: none -> 1.56 us  [hand_over(): pl.pallas_call(hand_over_kernel, out_shape=tuple((jax.ShapeDtypeStruct(r....]
where the time goes in v4:
time: 29.1 us; the launch traced here: 28.9 us
  Pallas kernels  27.6 us (95%)
  between operations  1.29 us (4%)
    pallas_call x1, Pallas kernels, layer(): pl.pallas_call(partial(layer_kernel, count, groups, tile, spread_ffn), ou...  26.1 us
    pallas_call x1, Pallas kernels, hand_over(): pl.pallas_call(hand_over_kernel, out_shape=tuple((jax.ShapeDtypeStruct(r....  1.56 us

profile of v4, /device:TPU:0, one launch (start us, length us, event | category | flops | bytes accessed | tf_op | source)
XLA Modules:
  0.0 28.9 jit_solution(8891846818082625191)
XLA Ops:
  1.3 26.1 %shard_map.211 = (bf16[1,800]{1,0:T(2,128)(2,1)}, bf16[1,640]{1,0:T(2,128)(2,1)}, f32[1,16,1600]{2,1,0:T(8,128)}) custom-call(bf16[1,1600]{1,0:T(2,128)(2,1)} %refs_0_.1, s32[1]{0:T(128)S(6)} %copy.23.refs_1_, s32[1,8]{1,0:T(1,128)} %refs_2_.1, f32[1,16,1600]{2,1,0:T(8,128)} %refs_3_.1, f32[1600]{0:T(1024)} %refs_4_.1, f32[1600]{0:T(1024)} %refs_5_.1, ...), custom_call_target="tpu_custom_call" | custom-call | tf_op jit(solution)/shard_map/pallas_call | solution.py:525
  27.4 1.6 %shard_map.212 = (bf16[1,800]{1,0:T(2,128)(2,1)}, bf16[1,640]{1,0:T(2,128)(2,1)}, f32[1,16,1600]{2,1,0:T(8,128)}) custom-call(bf16[1,800]{1,0:T(2,128)(2,1)} %get-tuple-element.6.row_in, bf16[1,640]{1,0:T(2,128)(2,1)} %get-tuple-element.7.fresh_in, f32[1,16,1600]{2,1,0:T(8,128)} %get-tuple-element.8.state_in), custom_call_target="tpu_custom_call" | custom-call | tf_op jit(solution)/shard_map/pallas_call | solution.py:480

commit v5 on v4

--- a/solution.py
+++ b/solution.py
@@ -123,13 +123,13 @@
     resid_ref, fresh_ref, new_state_ref = refs[:3]
     (
         keys_ref, values_ref, qkv_w, attn_w, mamba_w, select_w, step_w, out_w,
-        qkv_buf, sel_buf, stat_buf, mix_buf, load_sem, send_sem, recv_sem,
-    ) = refs[3:18]
+        qkv_buf, sel_buf, stat_buf, mix_buf, spread_ref, gather_ref, load_sem, send_sem, recv_sem,
+    ) = refs[3:20]
     if spread_ffn:
         (
             gate_up_w, down_w, gate_up_tail, down_tail, row_buf, rows_ref, part_buf, take_buf,
             far_send, far_recv,
-        ) = refs[18:]
+        ) = refs[20:]
     me = lax.axis_index("blk")
     width = hidden_ref.shape[1]
     channels = state_ref.shape[2]
@@ -222,9 +222,21 @@
                     barrier, inc=1, device_id=(lax.rem(grp + k, groups), b), device_id_type=MESH
                 )
 
-        pl.semaphore_wait(barrier, groups * count - 1)
-    else:
-        pl.semaphore_wait(barrier, count - 1)
+
+    part = att_width // count
+    def owner_column(flat):
+        head_group = jnp.zeros_like(flat)
+        for g in range(1, KEY_HEADS):
+            head_group = head_group + (flat >= g * group * HEAD_SIZE).astype(jnp.int32)
+        return head_group * HEAD_SIZE + (flat & (HEAD_SIZE - 1))
+
+    def selection(first, amount):
+        owner = owner_column(lax.broadcasted_iota(jnp.int32, (1, amount), 1) + first)
+        row = lax.broadcasted_iota(jnp.int32, (key_width, amount), 0)
+        return jnp.where(row == owner, 1.0, 0.0).astype(jnp.bfloat16)
+
+    spread_ref[...] = selection(0, att_width)
+    gather_ref[...] = selection(me * part, part)
 
     hidden_f = hidden_ref[...].astype(jnp.float32)
     normed_f = hidden_f * rms_scale(hidden_f) * norm_ref[...].reshape(1, width)
@@ -233,6 +245,7 @@
 
     load_qkv.wait()
     qkv_buf[me] = row_dot(own_feat, qkv_w[...])
+    pl.semaphore_wait(barrier, groups * count - 1 if spread_ffn else count - 1)
     sent_qkv = send_all(qkv_buf, send_sem, recv_sem, 0, count)
 
     def feature_dot(which, waits):
@@ -255,19 +268,10 @@
     new_key = qkv_f[:, att_width : att_width + key_width]
     new_value = qkv_f[:, att_width + key_width :]
 
-    def owner_column(flat):
-        head_group = jnp.zeros_like(flat)
-        for g in range(1, KEY_HEADS):
-            head_group = head_group + (flat >= g * group * HEAD_SIZE).astype(jnp.int32)
-        return head_group * HEAD_SIZE + (flat & (HEAD_SIZE - 1))
-
-    flat_rows = lax.broadcasted_iota(jnp.int32, (att_width, key_width), 0)
-    flat_cols = lax.broadcasted_iota(jnp.int32, (att_width, key_width), 1)
-    spread = (owner_column(flat_rows) == flat_cols).astype(jnp.float32).astype(jnp.bfloat16)
     head_of = lax.broadcasted_iota(jnp.int32, (HEAD_ROWS, att_width), 0)
     head_lane = lax.broadcasted_iota(jnp.int32, (HEAD_ROWS, att_width), 1)
     query_rows = jnp.where(head_of == (head_lane >> 6), jnp.broadcast_to(query, head_of.shape), 0.0)
-    query_f = bdot(query_rows.astype(jnp.bfloat16), spread)
+    query_f = bdot_t(query_rows.astype(jnp.bfloat16), spread_ref[...])
     query_bf = query_f.astype(jnp.bfloat16)
 
     scale = HEAD_SIZE ** (-0.5)
@@ -346,11 +350,7 @@
     for g in range(1, KEY_HEADS):
         att_group = att_group + (att_rows >= g * group).astype(jnp.int32)
     attended = jnp.where(att_group == att_cols, attended, 0.0).astype(jnp.bfloat16)
-    part = att_width // count
-    gather_rows = lax.broadcasted_iota(jnp.int32, (key_width, part), 0)
-    gather_cols = lax.broadcasted_iota(jnp.int32, (key_width, part), 1) + me * part
-    gather = (owner_column(gather_cols) == gather_rows).astype(jnp.float32).astype(jnp.bfloat16)
-    att_flat = bdot(attended, gather)
+    att_flat = bdot(attended, gather_ref[...])
     flat_head = lax.broadcasted_iota(jnp.int32, (HEAD_ROWS, part), 0)
     flat_lane = (lax.broadcasted_iota(jnp.int32, (HEAD_ROWS, part), 1) + me * part) >> 6
     own_att = jnp.sum(jnp.where(flat_head == flat_lane, att_flat, 0.0), axis=0, keepdims=True)
@@ -541,6 +541,8 @@
             pltpu.VMEM((count, 1, select_proj.shape[0]), jnp.float32),
             pltpu.VMEM((count, HEAD_ROWS, STAT_LANES), jnp.float32),
             pltpu.VMEM((count, 1, width), jnp.float32),
+            pltpu.VMEM((KEY_HEADS * HEAD_SIZE, QUERY_HEADS * HEAD_SIZE), jnp.bfloat16),
+            pltpu.VMEM((KEY_HEADS * HEAD_SIZE, QUERY_HEADS * HEAD_SIZE // count), jnp.bfloat16),
             pltpu.SemaphoreType.DMA((40,)),
             pltpu.SemaphoreType.DMA((4, count)),
             pltpu.SemaphoreType.DMA((4, count)),

time: 29.1 us -> 28.4 us (0.976)
  Pallas kernels: 27.6 us -> 26.9 us
    pallas_call x1, Pallas kernels: 26.1 us -> 25.4 us  [layer(): pl.pallas_call(partial(layer_kernel, count, groups, tile, spread_ffn), ou...]
where the time goes in v5:
time: 28.4 us; the launch traced here: 28.2 us
  Pallas kernels  26.9 us (95%)
  between operations  1.29 us (5%)
    pallas_call x1, Pallas kernels, layer(): pl.pallas_call(partial(layer_kernel, count, groups, tile, spread_ffn), ou...  25.4 us
    pallas_call x1, Pallas kernels, hand_over(): pl.pallas_call(hand_over_kernel, out_shape=tuple((jax.ShapeDtypeStruct(r....  1.56 us

profile of v5, /device:TPU:0, one launch (start us, length us, event | category | flops | bytes accessed | tf_op | source)
XLA Modules:
  0.0 28.2 jit_solution(17114379316178292062)
XLA Ops:
  1.3 25.4 %shard_map.211 = (bf16[1,800]{1,0:T(2,128)(2,1)}, bf16[1,640]{1,0:T(2,128)(2,1)}, f32[1,16,1600]{2,1,0:T(8,128)}) custom-call(bf16[1,1600]{1,0:T(2,128)(2,1)} %refs_0_.1, s32[1]{0:T(128)S(6)} %copy.23.refs_1_, s32[1,8]{1,0:T(1,128)} %refs_2_.1, f32[1,16,1600]{2,1,0:T(8,128)} %refs_3_.1, f32[1600]{0:T(1024)} %refs_4_.1, f32[1600]{0:T(1024)} %refs_5_.1, ...), custom_call_target="tpu_custom_call" | custom-call | tf_op jit(solution)/shard_map/pallas_call | solution.py:525
  26.7 1.6 %shard_map.212 = (bf16[1,800]{1,0:T(2,128)(2,1)}, bf16[1,640]{1,0:T(2,128)(2,1)}, f32[1,16,1600]{2,1,0:T(8,128)}) custom-call(bf16[1,800]{1,0:T(2,128)(2,1)} %get-tuple-element.6.row_in, bf16[1,640]{1,0:T(2,128)(2,1)} %get-tuple-element.7.fresh_in, f32[1,16,1600]{2,1,0:T(8,128)} %get-tuple-element.8.state_in), custom_call_target="tpu_custom_call" | custom-call | tf_op jit(solution)/shard_map/pallas_call | solution.py:480
